TPU v7x, 256 devices: a whole 4x4x8 slice. The times are simulated.
256 devices in a mesh: seq: 64 (over y_hi, z, x), ch: 4 (over y_lo, core).
Axes of the slice: x: 4, y: 4 (y_hi: 2, y_lo: 2; y = y_hi * 2 + y_lo), z: 8, core: 2. Of those that a mesh axis runs over, the one named last changes fastest.
Arguments:
- query_raw: bfloat16 [8192, 2048], P('seq', 'ch'), may hold values from -6 to 6
- key_raw: bfloat16 [8192, 2048], P('seq', 'ch'), may hold values from -6 to 6
- value_raw: bfloat16 [8192, 2048], P('seq', 'ch'), may hold values from -6 to 6
- featurizer: float32 [3, 7, 2048], P(None, None, 'ch'), may hold values from -2 to 2
- filter_taps: bfloat16 [8192, 2048], P(('seq', 'ch')), may hold values from -2.5 to 2.5
- cotangent: bfloat16 [8192, 2048], P('seq', 'ch'), may hold values from -6 to 6
Outputs:
- mixed: bfloat16 [8192, 2048], P('seq', 'ch')
- query_grad: bfloat16 [8192, 2048], P('seq', 'ch')
- key_grad: bfloat16 [8192, 2048], P('seq', 'ch')
- value_grad: bfloat16 [8192, 2048], P('seq', 'ch')
- filter_grad: float32 [8192, 2048], P(('seq', 'ch'))
- featurizer_grad: float32 [3, 7, 2048], P(None, None, 'ch')
All inputs are finite; a program needn't handle non-finite values.
Results may differ from a plain program's by a relative error of at most 0.0085.
Values may be sent and summed in bfloat16 or wider, within the bound.
No kernel may reach another device: no remote copies, remote signals or barrier semaphores. Data moves between devices by JAX's collectives and lax.ppermute only.
A program may use at most 64 MiB of HBM per device.

v0:
```python
import functools

import jax
import jax.numpy as jnp
from jax import lax
from jax.experimental import pallas as pl
from jax.experimental.pallas import tpu as pltpu
from jax.sharding import Mesh
from jax.sharding import PartitionSpec as P

TAPS = 7
SEQ = ("seq_0", "seq_1", "seq_2")
SEQ_CH = ("seq_0", "seq_1", "seq_2", "ch")
LANES = 128
OWN = 8
VMEM_LIMIT = 56 * 1024 * 1024

f32 = jnp.float32
bf16 = jnp.bfloat16


def pack_kernel(q_ref, k_ref, v_ref, c_ref, h_ref, out_ref):
    for index, ref in enumerate((q_ref, k_ref, v_ref, c_ref, h_ref)):
        turned = ref[...].astype(f32).T
        blocks = turned.reshape(turned.shape[0] // OWN, OWN, LANES)
        out_ref[:, index * OWN : (index + 1) * OWN, :] = blocks.astype(bf16)


def unpack_kernel(in_ref, mixed_ref, qg_ref, kg_ref, vg_ref, fg_ref, wg_ref):
    for index, ref in enumerate((mixed_ref, qg_ref, kg_ref, vg_ref, fg_ref)):
        blocks = in_ref[:, index * OWN : (index + 1) * OWN, :].astype(f32)
        rows = blocks.reshape(blocks.shape[0] * OWN, LANES)
        ref[...] = rows.T.astype(bf16)
    blocks = in_ref[:, 5 * OWN : 6 * OWN, :].astype(f32)
    sums = blocks.reshape(blocks.shape[0] * OWN, LANES).T
    wg_ref[...] = sums[0:24] + sums[32:56]


def backward_shifts(block, after_rolled, lane):
    rolled = [pltpu.roll(block, LANES - j, 1) for j in range(1, TAPS)]
    shifted = [
        jnp.where(lane < LANES - j, rolled[j - 1], after_rolled[j - 1]) for j in range(1, TAPS)
    ]
    return rolled, shifted


def owner_kernel(
    in_ref,
    w_ref,
    out_ref,
    fq_ref,
    fk_ref,
    fv_ref,
    mix_ref,
    gate_ref,
    tap_ref,
    xm_ref,
    xg_ref,
    xh_ref,
    res_ref,
    *,
    blocks,
    scale,
):
    lane = lax.broadcasted_iota(jnp.int32, (OWN, LANES), 1)
    flip_row = lax.broadcasted_iota(jnp.int32, (LANES, LANES), 0)
    flip_col = lax.broadcasted_iota(jnp.int32, (LANES, LANES), 1)
    flip = (flip_row + flip_col == LANES - 1).astype(f32).astype(bf16)
    zero = jnp.zeros((OWN, LANES), f32)

    def slab(s, index):
        return in_ref[s, index * OWN : (index + 1) * OWN, :].astype(f32)

    def forward(s, carry):
        feats = []
        after = []
        for index in range(3):
            block = slab(s, index)
            rolled = [pltpu.roll(block, j, 1) for j in range(1, TAPS)]
            total = w_ref[index * TAPS] * block
            for j in range(1, TAPS):
                shifted = jnp.where(lane >= j, rolled[j - 1], carry[index * (TAPS - 1) + j - 1])
                total = total + w_ref[index * TAPS + j] * shifted
            after += rolled
            feats.append(total)
        fq_ref[s], fk_ref[s], fv_ref[s] = feats
        rows = pl.ds(pl.multiple_of(s * OWN, OWN), OWN)
        mix_ref[rows, :] = (feats[1] * feats[2]).astype(bf16).astype(f32)
        gate_ref[rows, :] = (slab(s, 3) * feats[0]).astype(bf16).astype(f32)
        tap_ref[rows, :] = slab(s, 4)
        return tuple(after)

    lax.fori_loop(0, blocks, forward, (zero,) * (3 * (TAPS - 1)), unroll=2)

    res_ref[...] = jnp.dot(gate_ref[...].astype(bf16), flip, preferred_element_type=f32)

    @pl.loop(0, blocks)
    def _(s):
        rows = pl.ds(pl.multiple_of(s * OWN, OWN), OWN)
        back = pl.ds(pl.multiple_of((blocks - 1 - s) * OWN, OWN), OWN)
        gate_ref[rows, :] = res_ref[back, :]

    for r in range(OWN):
        for source, target in ((mix_ref, xm_ref), (gate_ref, xg_ref), (tap_ref, xh_ref)):
            target[r, :blocks, :] = jnp.zeros((blocks, LANES), f32)
            target[r, blocks:, :] = source[pl.ds(r, blocks, stride=OWN), :]

    wide_row = lax.broadcasted_iota(jnp.int32, (LANES, LANES), 0)
    wide_col = lax.broadcasted_iota(jnp.int32, (LANES, LANES), 1)
    causal = wide_col >= wide_row

    def long_conv(r, toeplitz_ref, operand_refs):
        before = jnp.zeros((LANES, LANES), f32)
        totals = [[None] * (blocks // 16) for _ in operand_refs]
        for pair in range(blocks // 2):
            tiles = []
            for d in (2 * pair, 2 * pair + 1):
                row = toeplitz_ref[r, blocks + d : blocks + d + 1, :]
                turned = pltpu.roll(
                    jnp.broadcast_to(row, (LANES, LANES)), 0, 1, stride=1, stride_axis=0
                )
                tiles.append(jnp.where(causal, turned, before).astype(bf16))
                before = turned
            right = jnp.concatenate(tiles, axis=0)
            first = (2 * pair) // 16
            for o, operand_ref in enumerate(operand_refs):
                left = jnp.concatenate(
                    [
                        operand_ref[r, blocks - d + 16 * first : 2 * blocks - d, :].astype(bf16)
                        for d in (2 * pair, 2 * pair + 1)
                    ],
                    axis=1,
                )
                product = jnp.dot(left, right, preferred_element_type=f32)
                for part in range(first, blocks // 16):
                    piece = product[16 * (part - first) : 16 * (part - first + 1)]
                    old = totals[o][part]
                    totals[o][part] = piece if old is None else old + piece
        return [jnp.concatenate(parts, axis=0) for parts in totals]

    @pl.loop(0, OWN)
    def _(r):
        (taps_sum,) = long_conv(r, xm_ref, (xg_ref,))
        tap_ref[pl.ds(r, blocks, stride=OWN), :] = taps_sum * scale

    @pl.loop(0, OWN)
    def _(r):
        conv, mix_grad = long_conv(r, xh_ref, (xm_ref, xg_ref))
        mix_ref[pl.ds(r, blocks, stride=OWN), :] = conv
        gate_ref[pl.ds(r, blocks, stride=OWN), :] = mix_grad

    res_ref[...] = jnp.dot(gate_ref[...].astype(bf16), flip, preferred_element_type=f32)
    gate_ref[...] = jnp.dot(tap_ref[...].astype(bf16), flip, preferred_element_type=f32)

    def backward(step, carry):
        s = blocks - 1 - step
        rows = pl.ds(pl.multiple_of(s * OWN, OWN), OWN)
        back = pl.ds(pl.multiple_of(step * OWN, OWN), OWN)
        conv = mix_ref[rows, :].astype(bf16).astype(f32)
        mix_grad = res_ref[back, :]
        upstream = slab(s, 3)
        grads = (upstream * conv, mix_grad * fv_ref[s], mix_grad * fk_ref[s])
        after, sums = carry
        new_after, new_sums = [], []
        outs = [fq_ref[s] * conv]
        for index in range(3):
            raw = slab(s, index)
            kept = after[index * (TAPS - 1) : (index + 1) * (TAPS - 1)]
            rolled, shifted = backward_shifts(grads[index], kept, lane)
            new_after += rolled
            total = w_ref[index * TAPS] * grads[index]
            new_sums.append(sums[index * TAPS] + raw * grads[index])
            for j in range(1, TAPS):
                total = total + w_ref[index * TAPS + j] * shifted[j - 1]
                new_sums.append(sums[index * TAPS + j] + raw * shifted[j - 1])
            outs.append(total)
        outs.append(gate_ref[back, :])
        for index, value in enumerate(outs):
            out_ref[s, index * OWN : (index + 1) * OWN, :] = value.astype(bf16)
        return tuple(new_after), tuple(new_sums)

    _, sums = lax.fori_loop(
        0, blocks, backward, ((zero,) * (3 * (TAPS - 1)), (zero,) * (3 * TAPS))
    )
    high = zero
    low = zero
    for index, value in enumerate(sums):
        total = jnp.sum(value, axis=1, keepdims=True) * scale
        coarse = total.astype(bf16).astype(f32)
        high = jnp.where(lane == index, coarse, high)
        low = jnp.where(lane == index + 32, total - coarse, low)
    packed = (high + low).astype(bf16)

    @pl.loop(0, blocks)
    def _(s):
        out_ref[s, 5 * OWN : 6 * OWN, :] = packed


def on_device(query_raw, key_raw, value_raw, featurizer, filter_taps, cotangent):
    tok_rows, channels = query_raw.shape
    seq_size = lax.axis_size(SEQ)
    ch_size = lax.axis_size("ch")
    me = lax.axis_index(SEQ)
    params = pltpu.CompilerParams(vmem_limit_bytes=VMEM_LIMIT)

    sub_rows = filter_taps.shape[0]
    taps_split = filter_taps.reshape(sub_rows, ch_size, channels).transpose(1, 0, 2)
    taps_rows = lax.all_to_all(taps_split, "ch", split_axis=0, concat_axis=0, tiled=True)
    taps_rows = taps_rows.reshape(tok_rows, channels)

    packed = pl.pallas_call(
        pack_kernel,
        out_shape=jax.ShapeDtypeStruct((seq_size, 5 * OWN, LANES), bf16),
        compiler_params=params,
        name="pack",
    )(query_raw, key_raw, value_raw, cotangent, taps_rows)
    received = lax.all_to_all(packed, SEQ, split_axis=0, concat_axis=0, tiled=True)

    own = lax.dynamic_slice(featurizer, (0, 0, me * OWN), (3, TAPS, OWN))
    own = jnp.broadcast_to(own.reshape(3 * TAPS, OWN, 1), (3 * TAPS, OWN, LANES))
    rows = seq_size * OWN
    flat = pltpu.VMEM((rows, LANES), f32)
    by_block = pltpu.VMEM((seq_size, OWN, LANES), f32)
    by_channel = pltpu.VMEM((OWN, 2 * seq_size, LANES), f32)
    outgoing = pl.pallas_call(
        functools.partial(owner_kernel, blocks=seq_size, scale=(seq_size * LANES) ** -0.5),
        out_shape=jax.ShapeDtypeStruct((seq_size, 6 * OWN, LANES), bf16),
        scratch_shapes=[by_block] * 3 + [flat] * 3 + [by_channel] * 3 + [flat],
        compiler_params=params,
        name="owner",
    )(received, own)
    returned = lax.all_to_all(outgoing, SEQ, split_axis=0, concat_axis=0, tiled=True)

    here = jax.ShapeDtypeStruct((tok_rows, channels), bf16)
    mixed, query_grad, key_grad, value_grad, taps_grad, weight_sums = pl.pallas_call(
        unpack_kernel,
        out_shape=(here,) * 5 + (jax.ShapeDtypeStruct((24, channels), f32),),
        compiler_params=params,
        name="unpack",
    )(returned)
    filter_grad = lax.all_to_all(
        taps_grad.reshape(ch_size, sub_rows, channels), "ch", split_axis=0, concat_axis=0, tiled=True
    )
    filter_grad = filter_grad.transpose(1, 0, 2).reshape(sub_rows, ch_size * channels).astype(f32)
    featurizer_grad = weight_sums[: 3 * TAPS].reshape(3, TAPS, channels)
    return mixed, query_grad, key_grad, value_grad, filter_grad, featurizer_grad


def solution(mesh):
    finer = Mesh(mesh.devices.reshape(2, 8, 4, mesh.shape["ch"]), ("seq_0", "seq_1", "seq_2", "ch"))
    placed = (
        P(SEQ, "ch"),
        P(SEQ, "ch"),
        P(SEQ, "ch"),
        P(None, None, "ch"),
        P(SEQ_CH, None),
        P(SEQ, "ch"),
    )
    return jax.shard_map(
        on_device,
        mesh=finer,
        in_specs=placed,
        out_specs=(
            P(SEQ, "ch"),
            P(SEQ, "ch"),
            P(SEQ, "ch"),
            P(SEQ, "ch"),
            P(SEQ_CH, None),
            P(None, None, "ch"),
        ),
        check_vma=False,
    )
```

profile of v0, /device:TPU:1, one launch (start us, length us, event | category | flops | bytes accessed | tf_op | source)
XLA Modules:
  0.0 114.6 jit_solution(1958118039065915479)
XLA Ops:
  0.6 0.0 copy-start
  0.6 0.9 copy.22
  1.6 9.9 %all_to_all.20 = bf16[4,32,512]{2,1,0:T(8,128)(2,1)} all-to-all(bf16[4,32,512]{2,1,0:T(8,128)(2,1)S(1)} %bitcast.15), channel_id=1, replica_groups=mesh['seq_0'=2,'seq_1'=8,'seq_2'=4,'ch'=4] {'ch'}, dimensions={0} | all-to-all | bytes 262144 | tf_op jit(solution)/shard_map/all_to_all | solution.py:208
  11.4 2.2 %pack.1 = bf16[64,40,128]{2,1,0:T(8,128)(2,1)} custom-call(bf16[128,512]{1,0:T(8,128)(2,1)} %q_ref.1, bf16[128,512]{1,0:T(8,128)(2,1)} %k_ref.1, bf16[128,512]{1,0:T(8,128)(2,1)} %v_ref.1, bf16[128,512]{1,0:T(8,128)(2,1)} %c_ref.1, bf16[128,512]{1,0:T(8,128)(2,1)} %bitcast.14), custom_call_target="tpu_custom_call" | custom-call | tf_op jit(solution)/shard_map/pack/pallas_call | solution.py:211
  13.7 12.6 %all-to-all-start.1 = ((bf16[64,40,128]{2,1,0:T(8,128)(2,1)}), bf16[64,40,128]{2,1,0:T(8,128)(2,1)S(1)}, u32[]{:S(2)}, u32[]{:S(2)}) async-start(bf16[64,40,128]{2,1,0:T(8,128)(2,1)} %pack.1), calls=%async_computation.1 | async-start | bytes 1310720 | tf_op jit(solution)/shard_map/all_to_all | solution.py:217
  26.3 0.0 copy-done
  26.3 0.1 constant_dynamic-slice_fusion
  26.3 19.8 %all-to-all-done.1.in_ref = bf16[64,40,128]{2,1,0:T(8,128)(2,1)S(1)} async-done(((bf16[64,40,128]{2,1,0:T(8,128)(2,1)}), bf16[64,40,128]{2,1,0:T(8,128)(2,1)S(1)}, u32[]{:S(2)}, u32[]{:S(2)}) %all-to-all-start.1) | async-done | bytes 655392 | tf_op jit(solution)/shard_map/all_to_all | solution.py:217
  46.1 0.0 copy-start.1
  46.1 0.8 broadcast_in_dim.8.w_ref
  47.0 0.1 copy-done.1
  47.0 25.4 %owner.1 = bf16[64,48,128]{2,1,0:T(8,128)(2,1)} custom-call(bf16[64,40,128]{2,1,0:T(8,128)(2,1)} %copy-done.1, f32[21,8,128]{2,1,0:T(8,128)} %broadcast_in_dim.8.w_ref), custom_call_target="tpu_custom_call" | custom-call | tf_op jit(solution)/shard_map/owner/pallas_call | solution.py:225
  72.4 29.2 %all_to_all.21.in_ref = bf16[64,48,128]{2,1,0:T(8,128)(2,1)} all-to-all(bf16[64,48,128]{2,1,0:T(8,128)(2,1)} %owner.1), channel_id=1, replica_groups=mesh['seq_0'=2,'seq_1'=8,'seq_2'=4,'ch'=4] {'seq_0','seq_1','seq_2'}, dimensions={0} | all-to-all | bytes 1572864 | tf_op jit(solution)/shard_map/all_to_all | solution.py:232
  101.6 2.1 %unpack.1 = (bf16[128,512]{1,0:T(8,128)(2,1)}, bf16[128,512]{1,0:T(8,128)(2,1)}, bf16[128,512]{1,0:T(8,128)(2,1)}, bf16[128,512]{1,0:T(8,128)(2,1)}, bf16[128,512]{1,0:T(8,128)(2,1)}, /*index=5*/f32[24,512]{1,0:T(8,128)}) custom-call(bf16[64,48,128]{2,1,0:T(8,128)(2,1)} %all_to_all.21.in_ref), custom_call_target="tpu_custom_call" | custom-call | tf_op jit(solution)/shard_map/unpack/pallas_call | solution.py:235
  103.6 0.0 copy-start.2
  103.6 6.6 %all-to-all-start.3 = ((bf16[4,32,512]{2,1,0:T(8,128)(2,1)}), bf16[4,32,512]{2,1,0:T(8,128)(2,1)S(1)}, u32[]{:S(2)}, u32[]{:S(2)}) async-start(bf16[4,32,512]{2,1,0:T(8,128)(2,1)} %bitcast.18), calls=%async_computation.3 | async-start | bytes 262144 | tf_op jit(solution)/shard_map/all_to_all | solution.py:241
  110.2 0.0 copy-done.2
  110.2 0.6 reshape.32
  110.9 3.0 %all-to-all-done.3 = bf16[4,32,512]{2,1,0:T(8,128)(2,1)S(1)} async-done(((bf16[4,32,512]{2,1,0:T(8,128)(2,1)}), bf16[4,32,512]{2,1,0:T(8,128)(2,1)S(1)}, u32[]{:S(2)}, u32[]{:S(2)}) %all-to-all-start.3) | async-done | bytes 131104 | tf_op jit(solution)/shard_map/all_to_all | solution.py:241
  113.9 0.7 copy.20
  (2 shorter events, 0.0 us)
Async XLA Ops:
  0.6 25.6 %copy-start = (f32[3,7,512]{2,1,0:T(8,128)S(1)}, f32[3,7,512]{2,1,0:T(8,128)}, u32[]{:S(2)}) copy-start(f32[3,7,512]{2,1,0:T(8,128)} %param.9) | copy-start | bytes 129028
  13.7 32.4 %all-to-all-start.1 = ((bf16[64,40,128]{2,1,0:T(8,128)(2,1)}), bf16[64,40,128]{2,1,0:T(8,128)(2,1)S(1)}, u32[]{:S(2)}, u32[]{:S(2)}) async-start(bf16[64,40,128]{2,1,0:T(8,128)(2,1)} %pack.1), calls=%async_computation.1 | async-start | bytes 1310720 | tf_op jit(solution)/shard_map/all_to_all | solution.py:217
  46.1 0.9 copy-start.1
  103.6 6.6 %copy-start.2 = (f32[24,512]{1,0:T(8,128)S(1)}, f32[24,512]{1,0:T(8,128)}, u32[]{:S(2)}) copy-start(f32[24,512]{1,0:T(8,128)} %get-tuple-element.17) | copy-start | bytes 147460
  103.6 10.2 %all-to-all-start.3 = ((bf16[4,32,512]{2,1,0:T(8,128)(2,1)}), bf16[4,32,512]{2,1,0:T(8,128)(2,1)S(1)}, u32[]{:S(2)}, u32[]{:S(2)}) async-start(bf16[4,32,512]{2,1,0:T(8,128)(2,1)} %bitcast.18), calls=%async_computation.3 | async-start | bytes 262144 | tf_op jit(solution)/shard_map/all_to_all | solution.py:241
where the time goes:
time: 115 us
  blocking collectives  39 us (34%)
  Pallas kernels  29.7 us (26%)
  waiting for transfers between devices  22.7 us (20%)
  starting transfers between devices  19.1 us (17%)
  local copies, waits for them, and re-layouts  3.27 us (3%)
    all_to_all x1, blocking collectives, on_device(): lax.all_to_all(outgoing, SEQ, split_axis=0, concat_axis=0, tiled=True)  29.2 us
    pallas_call x1, Pallas kernels, on_device(): pl.pallas_call(functools.partial(owner_kernel, blocks=seq_size, scale=(se...  25.4 us
    all_to_all x1, waiting for transfers between devices, on_device(): lax.all_to_all(packed, SEQ, split_axis=0, concat_axis=0, tiled=True)  19.8 us
    all_to_all x1, starting transfers between devices, on_device(): lax.all_to_all(packed, SEQ, split_axis=0, concat_axis=0, tiled=True)  12.6 us
    all_to_all x1, blocking collectives, on_device(): lax.all_to_all(taps_split, 'ch', split_axis=0, concat_axis=0, tiled=True)  9.87 us
    all_to_all x1, starting transfers between devices, on_device(): lax.all_to_all(taps_grad.reshape(ch_size, sub_rows, channels), 'ch', spli...  6.6 us
    all_to_all x1, waiting for transfers between devices, on_device(): lax.all_to_all(taps_grad.reshape(ch_size, sub_rows, channels), 'ch', spli...  2.97 us
  transfers between devices with their start and end apart: 2, of which 2 were waited for; matrix products, arithmetic and copies ran while one was open for 1% of the time, Pallas kernels for 0%

commit v1 on v0

--- a/solution.py
+++ b/solution.py
@@ -13,7 +13,7 @@
 SEQ_CH = ("seq_0", "seq_1", "seq_2", "ch")
 LANES = 128
 OWN = 8
-VMEM_LIMIT = 56 * 1024 * 1024
+MIB = 1024 * 1024
 
 f32 = jnp.float32
 bf16 = jnp.bfloat16
@@ -201,7 +201,8 @@
     seq_size = lax.axis_size(SEQ)
     ch_size = lax.axis_size("ch")
     me = lax.axis_index(SEQ)
-    params = pltpu.CompilerParams(vmem_limit_bytes=VMEM_LIMIT)
+    small = pltpu.CompilerParams(vmem_limit_bytes=8 * MIB)
+    large = pltpu.CompilerParams(vmem_limit_bytes=16 * MIB)
 
     sub_rows = filter_taps.shape[0]
     taps_split = filter_taps.reshape(sub_rows, ch_size, channels).transpose(1, 0, 2)
@@ -211,13 +212,13 @@
     packed = pl.pallas_call(
         pack_kernel,
         out_shape=jax.ShapeDtypeStruct((seq_size, 5 * OWN, LANES), bf16),
-        compiler_params=params,
+        compiler_params=small,
         name="pack",
     )(query_raw, key_raw, value_raw, cotangent, taps_rows)
-    received = lax.all_to_all(packed, SEQ, split_axis=0, concat_axis=0, tiled=True)
-
     own = lax.dynamic_slice(featurizer, (0, 0, me * OWN), (3, TAPS, OWN))
     own = jnp.broadcast_to(own.reshape(3 * TAPS, OWN, 1), (3 * TAPS, OWN, LANES))
+    packed, own = lax.optimization_barrier((packed, own))
+    received = lax.all_to_all(packed, SEQ, split_axis=0, concat_axis=0, tiled=True)
     rows = seq_size * OWN
     flat = pltpu.VMEM((rows, LANES), f32)
     by_block = pltpu.VMEM((seq_size, OWN, LANES), f32)
@@ -226,7 +227,7 @@
         functools.partial(owner_kernel, blocks=seq_size, scale=(seq_size * LANES) ** -0.5),
         out_shape=jax.ShapeDtypeStruct((seq_size, 6 * OWN, LANES), bf16),
         scratch_shapes=[by_block] * 3 + [flat] * 3 + [by_channel] * 3 + [flat],
-        compiler_params=params,
+        compiler_params=large,
         name="owner",
     )(received, own)
     returned = lax.all_to_all(outgoing, SEQ, split_axis=0, concat_axis=0, tiled=True)
@@ -235,7 +236,7 @@
     mixed, query_grad, key_grad, value_grad, taps_grad, weight_sums = pl.pallas_call(
         unpack_kernel,
         out_shape=(here,) * 5 + (jax.ShapeDtypeStruct((24, channels), f32),),
-        compiler_params=params,
+        compiler_params=small,
         name="unpack",
     )(returned)
     filter_grad = lax.all_to_all(

time: 115 us -> 110 us (0.957)
  blocking collectives: 39 us -> 61.1 us
  waiting for transfers between devices: 22.7 us -> 6.49 us
  starting transfers between devices: 19.1 us -> 13.1 us
  Pallas kernels: 29.7 us -> 24.5 us
    all_to_all x1, blocking collectives: 9.87 us -> 32.2 us  [on_device(): lax.all_to_all(packed, SEQ, split_axis=0, concat_axis=0, tiled=True)]
    all_to_all x1, waiting for transfers between devices: 19.8 us -> 3.52 us  [on_device(): lax.all_to_all(taps_split, 'ch', split_axis=0, concat_axis=0, tiled=True)]
    all_to_all x1, starting transfers between devices: 12.6 us -> 6.66 us  [on_device(): lax.all_to_all(taps_split, 'ch', split_axis=0, concat_axis=0, tiled=True)]
    pallas_call x1, Pallas kernels: 25.4 us -> 23.3 us  [on_device(): pl.pallas_call(functools.partial(owner_kernel, blocks=seq_size, scale=(se...]
    pallas_call x1, Pallas kernels: 2.24 us -> 0.24 us  [on_device(): pl.pallas_call(pack_kernel, out_shape=jax.ShapeDtypeStruct((seq_size, 5 *...]
where the time goes in v1:
time: 110 us; the launch traced here: 109 us
  blocking collectives  61.1 us (56%)
  Pallas kernels  24.5 us (22%)
  starting transfers between devices  13.1 us (12%)
  waiting for transfers between devices  6.49 us (6%)
  local copies, waits for them, and re-layouts  3.14 us (3%)
    all_to_all x1, blocking collectives, on_device(): lax.all_to_all(packed, SEQ, split_axis=0, concat_axis=0, tiled=True)  32.2 us
    all_to_all x1, blocking collectives, on_device(): lax.all_to_all(outgoing, SEQ, split_axis=0, concat_axis=0, tiled=True)  28.9 us
    pallas_call x1, Pallas kernels, on_device(): pl.pallas_call(functools.partial(owner_kernel, blocks=seq_size, scale=(se...  23.3 us
    all_to_all x1, starting transfers between devices, on_device(): lax.all_to_all(taps_split, 'ch', split_axis=0, concat_axis=0, tiled=True)  6.66 us
    all_to_all x1, starting transfers between devices, on_device(): lax.all_to_all(taps_grad.reshape(ch_size, sub_rows, channels), 'ch', spli...  6.47 us
    all_to_all x1, waiting for transfers between devices, on_device(): lax.all_to_all(taps_split, 'ch', split_axis=0, concat_axis=0, tiled=True)  3.52 us
    all_to_all x1, waiting for transfers between devices, on_device(): lax.all_to_all(taps_grad.reshape(ch_size, sub_rows, channels), 'ch', spli...  2.97 us
  transfers between devices with their start and end apart: 2, of which 2 were waited for; matrix products, arithmetic and copies ran while one was open for 1% of the time, Pallas kernels for 0%

profile of v1, /device:TPU:1, one launch (start us, length us, event | category | flops | bytes accessed | tf_op | source)
XLA Modules:
  0.0 109.1 jit_solution(11301192951200162212)
XLA Ops:
  0.6 0.0 copy-start
  0.6 0.0 copy-start.3
  0.7 0.0 copy-start.4
  0.7 1.6 %copy.22 = bf16[4,4,8,512]{3,2,0,1:T(8,128)(2,1)} copy(bf16[4,4,8,512]{3,2,1,0:T(8,128)(2,1)} %bitcast.17) | data formatting | bytes 262144 | tf_op jit(solution)/shard_map/reshape | solution.py:208
  2.3 0.0 copy-start.1
  2.3 0.0 copy-start.2
  2.3 6.7 %all-to-all-start = ((bf16[4,32,512]{2,1,0:T(8,128)(2,1)}), bf16[4,32,512]{2,1,0:T(8,128)(2,1)S(1)}, u32[]{:S(2)}, u32[]{:S(2)}) async-start(bf16[4,32,512]{2,1,0:T(8,128)(2,1)} %bitcast.12), calls=%async_computation | async-start | bytes 262144 | tf_op jit(solution)/shard_map/all_to_all | solution.py:209
  8.9 0.0 copy-done
  9.0 0.1 constant_dynamic-slice_fusion
  9.0 3.5 %all-to-all-done = bf16[4,32,512]{2,1,0:T(8,128)(2,1)S(1)} async-done(((bf16[4,32,512]{2,1,0:T(8,128)(2,1)}), bf16[4,32,512]{2,1,0:T(8,128)(2,1)S(1)}, u32[]{:S(2)}, u32[]{:S(2)}) %all-to-all-start) | async-done | bytes 131104 | tf_op jit(solution)/shard_map/all_to_all | solution.py:209
  12.5 0.0 copy-done.3
  12.5 0.0 copy-done.4
  12.6 0.0 copy-done.1
  12.6 0.0 copy-done.2
  12.6 0.2 pack.1
  12.8 0.1 broadcast_in_dim.8.w_ref
  12.9 32.2 %all_to_all.20.in_ref = bf16[64,40,128]{2,1,0:T(8,128)(2,1)S(1)} all-to-all(bf16[64,40,128]{2,1,0:T(8,128)(2,1)S(1)} %pack.1), channel_id=1, replica_groups=mesh['seq_0'=2,'seq_1'=8,'seq_2'=4,'ch'=4] {'seq_0','seq_1','seq_2'}, dimensions={0} | all-to-all | bytes 1310720 | tf_op jit(solution)/shard_map/all_to_all | solution.py:221
  45.1 23.3 %owner.1 = bf16[64,48,128]{2,1,0:T(8,128)(2,1)S(1)} custom-call(bf16[64,40,128]{2,1,0:T(8,128)(2,1)S(1)} %all_to_all.20.in_ref, f32[21,8,128]{2,1,0:T(8,128)S(1)} %broadcast_in_dim.8.w_ref), custom_call_target="tpu_custom_call" | custom-call | tf_op jit(solution)/shard_map/owner/pallas_call | solution.py:226
  68.5 28.9 %all_to_all.21.in_ref = bf16[64,48,128]{2,1,0:T(8,128)(2,1)S(1)} all-to-all(bf16[64,48,128]{2,1,0:T(8,128)(2,1)S(1)} %owner.1), channel_id=1, replica_groups=mesh['seq_0'=2,'seq_1'=8,'seq_2'=4,'ch'=4] {'seq_0','seq_1','seq_2'}, dimensions={0} | all-to-all | bytes 1572864 | tf_op jit(solution)/shard_map/all_to_all | solution.py:233
  97.3 0.9 unpack.1
  98.2 6.5 %all-to-all-start.3 = ((bf16[4,32,512]{2,1,0:T(8,128)(2,1)}), bf16[4,32,512]{2,1,0:T(8,128)(2,1)S(1)}, u32[]{:S(2)}, u32[]{:S(2)}) async-start(bf16[4,32,512]{2,1,0:T(8,128)(2,1)} %bitcast.2), calls=%async_computation.3 | async-start | bytes 262144 | tf_op jit(solution)/shard_map/all_to_all | solution.py:242
  104.7 0.6 reshape.32
  105.3 3.0 %all-to-all-done.3 = bf16[4,32,512]{2,1,0:T(8,128)(2,1)S(1)} async-done(((bf16[4,32,512]{2,1,0:T(8,128)(2,1)}), bf16[4,32,512]{2,1,0:T(8,128)(2,1)S(1)}, u32[]{:S(2)}, u32[]{:S(2)}) %all-to-all-start.3) | async-done | bytes 131104 | tf_op jit(solution)/shard_map/all_to_all | solution.py:242
  108.3 0.7 copy.20
  (2 shorter events, 0.0 us)
Async XLA Ops:
  0.6 8.3 %copy-start = (f32[3,7,512]{2,1,0:T(8,128)S(1)}, f32[3,7,512]{2,1,0:T(8,128)}, u32[]{:S(2)}) copy-start(f32[3,7,512]{2,1,0:T(8,128)} %param.9) | copy-start | bytes 129028
  0.6 11.9 %copy-start.3 = (bf16[128,512]{1,0:T(8,128)(2,1)S(1)}, bf16[128,512]{1,0:T(8,128)(2,1)}, u32[]{:S(2)}) copy-start(bf16[128,512]{1,0:T(8,128)(2,1)} %v_ref.1) | copy-start | bytes 393220
  0.7 11.9 %copy-start.4 = (bf16[128,512]{1,0:T(8,128)(2,1)S(1)}, bf16[128,512]{1,0:T(8,128)(2,1)}, u32[]{:S(2)}) copy-start(bf16[128,512]{1,0:T(8,128)(2,1)} %c_ref.1) | copy-start | bytes 393220
  2.3 10.3 %copy-start.1 = (bf16[128,512]{1,0:T(8,128)(2,1)S(1)}, bf16[128,512]{1,0:T(8,128)(2,1)}, u32[]{:S(2)}) copy-start(bf16[128,512]{1,0:T(8,128)(2,1)} %q_ref.1) | copy-start | bytes 393220
  2.3 10.3 %copy-start.2 = (bf16[128,512]{1,0:T(8,128)(2,1)S(1)}, bf16[128,512]{1,0:T(8,128)(2,1)}, u32[]{:S(2)}) copy-start(bf16[128,512]{1,0:T(8,128)(2,1)} %k_ref.1) | copy-start | bytes 393220
  2.3 10.3 %all-to-all-start = ((bf16[4,32,512]{2,1,0:T(8,128)(2,1)}), bf16[4,32,512]{2,1,0:T(8,128)(2,1)S(1)}, u32[]{:S(2)}, u32[]{:S(2)}) async-start(bf16[4,32,512]{2,1,0:T(8,128)(2,1)} %bitcast.12), calls=%async_computation | async-start | bytes 262144 | tf_op jit(solution)/shard_map/all_to_all | solution.py:209
  98.2 10.1 %all-to-all-start.3 = ((bf16[4,32,512]{2,1,0:T(8,128)(2,1)}), bf16[4,32,512]{2,1,0:T(8,128)(2,1)S(1)}, u32[]{:S(2)}, u32[]{:S(2)}) async-start(bf16[4,32,512]{2,1,0:T(8,128)(2,1)} %bitcast.2), calls=%async_computation.3 | async-start | bytes 262144 | tf_op jit(solution)/shard_map/all_to_all | solution.py:242

commit v2 on v1

v2 whole, which is shorter than its diff:
```python
import functools

import jax
import jax.numpy as jnp
from jax import lax
from jax.experimental import pallas as pl
from jax.experimental.pallas import tpu as pltpu
from jax.sharding import Mesh
from jax.sharding import PartitionSpec as P

TAPS = 7
SEQ = ("seq_0", "seq_1", "seq_2")
SEQ_CH = ("seq_0", "seq_1", "seq_2", "ch")
LANES = 128
OWN = 8
GROUPS = 4
PIECE = LANES // GROUPS
WIDTH = 11 * LANES
MIB = 1024 * 1024

f32 = jnp.float32
bf16 = jnp.bfloat16


def pack_kernel(q_ref, k_ref, v_ref, c_ref, h_ref, w_ref, out_ref, weight_ref):
    half = out_ref.shape[0]
    rows = [ref[...].astype(f32) for ref in (q_ref, k_ref, v_ref, c_ref)]
    taps = h_ref[...].astype(f32)
    wide = 2 * half
    rows.append(jnp.concatenate([taps[:, g * wide : (g + 1) * wide] for g in range(GROUPS)], axis=0))
    for index, value in enumerate(rows):
        turned = value.T.astype(bf16)
        for e in range(2):
            column = (2 * index + e) * LANES
            out_ref[:, column : column + LANES] = turned[e * half : (e + 1) * half]
    weight_ref[...] = jnp.zeros_like(weight_ref)
    for index in range(3):
        weight = w_ref[index]
        coarse = weight.astype(bf16).astype(f32)
        for e in range(2):
            part = slice(e * half, (e + 1) * half)
            row = 64 * e + TAPS * index
            weight_ref[row : row + TAPS, :] = coarse[:, part]
            weight_ref[row + 32 : row + 32 + TAPS, :] = (weight - coarse)[:, part]
    out_ref[:, 10 * LANES :] = weight_ref[...].T.astype(bf16)


def unpack_kernel(in_ref, mixed_ref, qg_ref, kg_ref, vg_ref, fg_ref, wg_ref):
    half = in_ref.shape[0]

    def turned(index, e):
        column = (2 * index + e) * LANES
        return in_ref[:, column : column + LANES].astype(f32).T

    for e in range(2):
        part = slice(e * half, (e + 1) * half)
        for index, ref in enumerate((mixed_ref, qg_ref, kg_ref, vg_ref)):
            ref[:, part] = turned(index, e).astype(bf16)
        taps_grad = turned(4, e)
        for g in range(GROUPS):
            column = g * 2 * half + e * half
            fg_ref[:, column : column + half] = taps_grad[g * PIECE : (g + 1) * PIECE]
    sums = in_ref[:, 10 * LANES :].astype(f32).T
    for e in range(2):
        part = slice(e * half, (e + 1) * half)
        total = sums[64 * e : 64 * e + 24] + sums[64 * e + 32 : 64 * e + 56]
        for index in range(3):
            wg_ref[index, :, part] = total[TAPS * index : TAPS * (index + 1)]


def owner_kernel(
    in_ref,
    out_ref,
    w_ref,
    raw_ref,
    feat_ref,
    mix_ref,
    gate_ref,
    tap_ref,
    xm_ref,
    xg_ref,
    xh_ref,
    res_ref,
    *,
    blocks,
    scale,
):
    lane = lax.broadcasted_iota(jnp.int32, (OWN, LANES), 1)
    row = lax.broadcasted_iota(jnp.int32, (OWN, LANES), 0)
    first_half = row < GROUPS
    group = row % GROUPS
    piece = lane // PIECE
    flip_row = lax.broadcasted_iota(jnp.int32, (LANES, LANES), 0)
    flip_col = lax.broadcasted_iota(jnp.int32, (LANES, LANES), 1)
    flip = (flip_row + flip_col == LANES - 1).astype(f32).astype(bf16)
    zero = jnp.zeros((OWN, LANES), f32)
    steps = blocks // 4

    def half_turn(value):
        return pltpu.roll(value, GROUPS, 0)

    def regroup(one, two):
        return (
            jnp.where(first_half, one, half_turn(two)),
            jnp.where(first_half, half_turn(one), two),
        )

    def swap_pieces(value):
        result = value
        for k in range(1, GROUPS):
            moved = pltpu.roll(value, PIECE * k, 1)
            up = pltpu.roll(moved, OWN - k, 0)
            down = pltpu.roll(moved, GROUPS - k, 0)
            taken = jnp.where(group + k < GROUPS, up, down)
            result = jnp.where(piece == (group + k) % GROUPS, taken, result)
        return result

    def block_rows(s):
        return pl.ds(pl.multiple_of(s * OWN, OWN), OWN)

    weights = in_ref[0:OWN, 10 * LANES :].astype(f32)
    weights = jnp.where(first_half, weights, pltpu.roll(weights, 64, 1))
    weights = weights + pltpu.roll(weights, LANES - 32, 1)
    for index in range(3 * TAPS):
        w_ref[index] = jnp.broadcast_to(weights[:, index : index + 1], (OWN, LANES))

    @pl.loop(0, steps)
    def _(step):
        rows = pl.ds(pl.multiple_of(step * 16, 16), 16)
        for index in range(5):
            one = in_ref[rows, 2 * index * LANES : (2 * index + 1) * LANES].astype(f32)
            two = in_ref[rows, (2 * index + 1) * LANES : (2 * index + 2) * LANES].astype(f32)
            for part in range(2):
                pair = regroup(one[part * OWN : (part + 1) * OWN], two[part * OWN : (part + 1) * OWN])
                for which, value in enumerate(pair):
                    s = step * 4 + part * 2 + which
                    if index < 4:
                        raw_ref[index, s] = value
                    else:
                        tap_ref[block_rows(s), :] = swap_pieces(value)

    for index in range(3):

        def forward(step, kept, index=index):
            for which in range(4):
                s = step * 4 + which
                block = raw_ref[index, s]
                rolled = tuple(pltpu.roll(block, j, 1) for j in range(1, TAPS))
                total = w_ref[index * TAPS] * block
                for j in range(1, TAPS):
                    shifted = jnp.where(lane >= j, rolled[j - 1], kept[j - 1])
                    total = total + w_ref[index * TAPS + j] * shifted
                kept = rolled
                feat_ref[index, s] = total
                if index == 0:
                    gate_ref[block_rows(s), :] = (raw_ref[3, s] * total).astype(bf16).astype(f32)
                if index == 2:
                    mix_ref[block_rows(s), :] = (feat_ref[1, s] * total).astype(bf16).astype(f32)
            return kept

        lax.fori_loop(0, steps, forward, (zero,) * (TAPS - 1))

    res_ref[...] = jnp.dot(gate_ref[...].astype(bf16), flip, preferred_element_type=f32)

    @pl.loop(0, blocks)
    def _(s):
        gate_ref[block_rows(s), :] = res_ref[block_rows(blocks - 1 - s), :]

    for r in range(OWN):
        for source, target in ((mix_ref, xm_ref), (gate_ref, xg_ref), (tap_ref, xh_ref)):
            target[r, :blocks, :] = jnp.zeros((blocks, LANES), f32)
            target[r, blocks:, :] = source[pl.ds(r, blocks, stride=OWN), :]

    causal = flip_col >= flip_row

    def long_conv(r, toeplitz_ref, operand_refs):
        before = jnp.zeros((LANES, LANES), f32)
        totals = [[None] * (blocks // 16) for _ in operand_refs]
        for pair in range(blocks // 2):
            tiles = []
            for d in (2 * pair, 2 * pair + 1):
                line = toeplitz_ref[r, blocks + d : blocks + d + 1, :]
                turned = pltpu.roll(
                    jnp.broadcast_to(line, (LANES, LANES)), 0, 1, stride=1, stride_axis=0
                )
                tiles.append(jnp.where(causal, turned, before).astype(bf16))
                before = turned
            right = jnp.concatenate(tiles, axis=0)
            first = (2 * pair) // 16
            for o, operand_ref in enumerate(operand_refs):
                left = jnp.concatenate(
                    [
                        operand_ref[r, blocks - d + 16 * first : 2 * blocks - d, :].astype(bf16)
                        for d in (2 * pair, 2 * pair + 1)
                    ],
                    axis=1,
                )
                product = jnp.dot(left, right, preferred_element_type=f32)
                for part in range(first, blocks // 16):
                    added = product[16 * (part - first) : 16 * (part - first + 1)]
                    old = totals[o][part]
                    totals[o][part] = added if old is None else old + added
        return [jnp.concatenate(parts, axis=0) for parts in totals]

    @pl.loop(0, OWN)
    def _(r):
        (taps_sum,) = long_conv(r, xm_ref, (xg_ref,))
        tap_ref[pl.ds(r, blocks, stride=OWN), :] = taps_sum * scale

    @pl.loop(0, OWN)
    def _(r):
        conv, mix_grad = long_conv(r, xh_ref, (xm_ref, xg_ref))
        mix_ref[pl.ds(r, blocks, stride=OWN), :] = conv
        gate_ref[pl.ds(r, blocks, stride=OWN), :] = mix_grad

    res_ref[...] = jnp.dot(gate_ref[...].astype(bf16), flip, preferred_element_type=f32)
    gate_ref[...] = jnp.dot(tap_ref[...].astype(bf16), flip, preferred_element_type=f32)

    def put(step, index, values):
        ones, twos = zip(regroup(values[0], values[1]), regroup(values[2], values[3]))
        rows = pl.ds(pl.multiple_of(step * 16, 16), 16)
        for e, halves in enumerate((ones, twos)):
            column = (2 * index + e) * LANES
            out_ref[rows, column : column + LANES] = jnp.concatenate(halves, axis=0).astype(bf16)

    def back_block(s):
        return block_rows(blocks - 1 - s)

    @pl.loop(0, steps)
    def _(step):
        mixed, taps_grad = [], []
        for which in range(4):
            s = step * 4 + which
            conv = mix_ref[block_rows(s), :].astype(bf16).astype(f32)
            mix_ref[block_rows(s), :] = conv
            mixed.append(feat_ref[0, s] * conv)
            taps_grad.append(swap_pieces(gate_ref[back_block(s), :]))
        put(step, 0, mixed)
        put(step, 4, taps_grad)

    all_sums = []
    for index in range(3):

        def backward(count, carry, index=index):
            step = steps - 1 - count
            kept, sums = carry
            grads = [None] * 4
            for which in (3, 2, 1, 0):
                s = step * 4 + which
                if index == 0:
                    grad = raw_ref[3, s] * mix_ref[block_rows(s), :]
                else:
                    grad = res_ref[back_block(s), :] * feat_ref[3 - index, s]
                raw = raw_ref[index, s]
                rolled = tuple(pltpu.roll(grad, LANES - j, 1) for j in range(1, TAPS))
                total = w_ref[index * TAPS] * grad
                new_sums = [sums[0] + raw * grad]
                for j in range(1, TAPS):
                    shifted = jnp.where(lane < LANES - j, rolled[j - 1], kept[j - 1])
                    total = total + w_ref[index * TAPS + j] * shifted
                    new_sums.append(sums[j] + raw * shifted)
                kept, sums = rolled, tuple(new_sums)
                grads[which] = total
            put(step, index + 1, grads)
            return kept, sums

        _, sums = lax.fori_loop(0, steps, backward, ((zero,) * (TAPS - 1), (zero,) * TAPS))
        all_sums += sums

    high = zero
    low = zero
    for index, value in enumerate(all_sums):
        total = jnp.sum(value, axis=1, keepdims=True) * scale
        coarse = total.astype(bf16).astype(f32)
        high = jnp.where(lane == index, coarse, high)
        low = jnp.where(lane == index + 32, total - coarse, low)
    both = high + low
    both = jnp.where(lane < 64, both, pltpu.roll(half_turn(both), 64, 1))
    both = jnp.where(first_half, both, half_turn(both))
    both = jnp.concatenate([both, both], axis=0).astype(bf16)

    @pl.loop(0, steps)
    def _(step):
        out_ref[pl.ds(pl.multiple_of(step * 16, 16), 16), 10 * LANES :] = both


def on_device(query_raw, key_raw, value_raw, featurizer, filter_taps, cotangent):
    tok_rows, channels = query_raw.shape
    blocks = lax.axis_size(SEQ)
    devices = lax.axis_size(SEQ_CH)
    small = pltpu.CompilerParams(vmem_limit_bytes=12 * MIB)
    large = pltpu.CompilerParams(vmem_limit_bytes=20 * MIB)
    sent = jax.ShapeDtypeStruct((devices, WIDTH), bf16)

    packed = pl.pallas_call(
        pack_kernel,
        out_shape=sent,
        scratch_shapes=[pltpu.VMEM((LANES, devices), f32)],
        compiler_params=small,
        name="pack",
    )(query_raw, key_raw, value_raw, cotangent, filter_taps, featurizer)
    received = lax.all_to_all(packed, SEQ_CH, split_axis=0, concat_axis=0, tiled=True)

    flat = pltpu.VMEM((blocks * OWN, LANES), f32)
    by_channel = pltpu.VMEM((OWN, 2 * blocks, LANES), f32)
    outgoing = pl.pallas_call(
        functools.partial(owner_kernel, blocks=blocks, scale=(blocks * LANES) ** -0.5),
        out_shape=sent,
        scratch_shapes=[
            pltpu.VMEM((3 * TAPS, OWN, LANES), f32),
            pltpu.VMEM((4, blocks, OWN, LANES), f32),
            pltpu.VMEM((3, blocks, OWN, LANES), f32),
            flat,
            flat,
            flat,
            by_channel,
            by_channel,
            by_channel,
            flat,
        ],
        compiler_params=large,
        name="owner",
    )(received)
    returned = lax.all_to_all(outgoing, SEQ_CH, split_axis=0, concat_axis=0, tiled=True)

    here = jax.ShapeDtypeStruct((tok_rows, channels), bf16)
    return pl.pallas_call(
        unpack_kernel,
        out_shape=(here,) * 4
        + (
            jax.ShapeDtypeStruct(filter_taps.shape, f32),
            jax.ShapeDtypeStruct(featurizer.shape, f32),
        ),
        compiler_params=small,
        name="unpack",
    )(returned)


def solution(mesh):
    finer = Mesh(mesh.devices.reshape(2, 8, 4, mesh.shape["ch"]), ("seq_0", "seq_1", "seq_2", "ch"))
    placed = (
        P(SEQ, "ch"),
        P(SEQ, "ch"),
        P(SEQ, "ch"),
        P(None, None, "ch"),
        P(SEQ_CH, None),
        P(SEQ, "ch"),
    )
    return jax.shard_map(
        on_device,
        mesh=finer,
        in_specs=placed,
        out_specs=(
            P(SEQ, "ch"),
            P(SEQ, "ch"),
            P(SEQ, "ch"),
            P(SEQ, "ch"),
            P(SEQ_CH, None),
            P(None, None, "ch"),
        ),
        check_vma=False,
    )
```

time: 110 us -> 113 us (1.027)
  starting transfers between devices: 13.1 us -> 0 us
  blocking collectives: 61.1 us -> 72.7 us
  waiting for transfers between devices: 6.49 us -> 0 us
  local copies, waits for them, and re-layouts: 3.14 us -> 9.48 us
  Pallas kernels: 24.5 us -> 28 us
  other arithmetic: 0.02 us -> 2.3 us
    all_to_all x2 -> x0, starting transfers between devices: 13.1 us -> none  [the longest x1 6.66 us: on_device(): lax.all_to_all(taps_split, 'ch', split_axis=0, concat_axis=0, tiled=True)]
    all_to_all x2, blocking collectives: 61.1 us -> 72.7 us  [the longest x1 40.9 us: on_device(): lax.all_to_all(packed, SEQ_CH, split_axis=0, concat_axis=0, tiled=True)]
    unnamed x10 -> x18, local copies, waits for them, and re-layouts: 0.03 us -> 8.97 us
    all_to_all x2 -> x0, waiting for transfers between devices: 6.49 us -> none  [the longest x1 3.52 us: on_device(): lax.all_to_all(taps_split, 'ch', split_axis=0, concat_axis=0, tiled=True)]
    pallas_call x3, Pallas kernels: 24.5 us -> 28 us  [the longest x1 26.6 us: on_device(): pl.pallas_call(functools.partial(owner_kernel, blocks=blocks, scale=(bloc...]
    all_to_all x0 -> x2, other arithmetic: none -> 2.3 us  [the longest x1 1.15 us: on_device(): lax.all_to_all(outgoing, SEQ_CH, split_axis=0, concat_axis=0, tiled=True)]
    reshape x2 -> x0, local copies, waits for them, and re-layouts: 2.24 us -> none  [the longest x1 1.61 us: on_device(): filter_taps.reshape(sub_rows, ch_size, channels).transpose(1, 0, 2)]
  transfers between devices with their start and end apart: 2 -> 0, of which waited for: 2 -> 0; matrix products, arithmetic and copies ran while one was open for 1% -> 0% of each run, Pallas kernels for 0% -> 0%
where the time goes in v2:
time: 113 us
  blocking collectives  72.7 us (64%)
  Pallas kernels  28 us (25%)
  local copies, waits for them, and re-layouts  9.48 us (8%)
  other arithmetic  2.3 us (2%)
    all_to_all x1, blocking collectives, on_device(): lax.all_to_all(packed, SEQ_CH, split_axis=0, concat_axis=0, tiled=True)  40.9 us
    all_to_all x1, blocking collectives, on_device(): lax.all_to_all(outgoing, SEQ_CH, split_axis=0, concat_axis=0, tiled=True)  31.8 us
    pallas_call x1, Pallas kernels, on_device(): pl.pallas_call(functools.partial(owner_kernel, blocks=blocks, scale=(bloc...  26.6 us
    unnamed x18, local copies, waits for them, and re-layouts  8.97 us

profile of v2, /device:TPU:1, one launch (start us, length us, event | category | flops | bytes accessed | tf_op | source)
XLA Modules:
  0.0 113.1 jit_solution(12632686320972973890)
XLA Ops:
  0.6 0.0 copy-start
  0.6 0.9 copy-done
  1.5 0.0 copy-start.1
  1.5 0.9 copy-done.1
  2.4 0.0 copy-start.2
  2.4 0.9 copy-done.2
  3.3 0.0 copy-start.3
  3.4 0.9 copy-done.3
  4.3 0.0 copy-start.4
  4.3 0.9 copy-done.4
  5.2 0.0 copy-start.5
  5.2 0.8 copy-done.5
  6.0 0.3 pack.1
  6.2 0.5 broadcast
  6.7 1.1 %reduce = bf16[256,1408]{1,0:T(8,128)(2,1)S(1)} reduce(bf16[256,1,1408]{2,0,1:T(8,128)(2,1)S(1)} %bitcast.10, bf16[]{:T(256)} %broadcast), dimensions={1}, to_apply=%copy.14.reduce_sub_computation | reduce | bytes 1441794 | tf_op jit(solution)/shard_map/all_to_all | solution.py:302
  7.9 0.8 reshape.16
  8.7 40.9 %all_to_all.22 = bf16[256,2,704]{2,1,0:T(2,128)(2,1)S(1)} all-to-all(bf16[256,2,704]{2,1,0:T(2,128)(2,1)S(1)} %reshape.16), channel_id=1, replica_groups=mesh['seq_0'=2,'seq_1'=8,'seq_2'=4,'ch'=4] {'seq_0','seq_1','seq_2','ch'}, dimensions={0} | all-to-all | bytes 1441792 | tf_op jit(solution)/shard_map/all_to_all | solution.py:302
  49.6 1.0 reshape.17
  50.6 0.1 copy.21
  50.7 26.6 %owner.1 = bf16[256,1408]{1,0:T(8,128)(2,1)S(1)} custom-call(bf16[256,1408]{1,0:T(8,128)(2,1)S(1)} %bitcast.9), custom_call_target="tpu_custom_call" | custom-call | tf_op jit(solution)/shard_map/owner/pallas_call | solution.py:306
  77.3 1.1 %reduce.1 = bf16[256,1408]{1,0:T(8,128)(2,1)S(1)} reduce(bf16[256,1,1408]{2,0,1:T(8,128)(2,1)S(1)} %bitcast.11, bf16[]{:T(256)} %broadcast), dimensions={1}, to_apply=%copy.15.reduce_sub_computation | reduce | bytes 1441794 | tf_op jit(solution)/shard_map/all_to_all | solution.py:324
  78.5 0.8 reshape.18
  79.2 31.8 %all_to_all.23 = bf16[256,2,704]{2,1,0:T(2,128)(2,1)S(1)} all-to-all(bf16[256,2,704]{2,1,0:T(2,128)(2,1)S(1)} %reshape.18), channel_id=1, replica_groups=mesh['seq_0'=2,'seq_1'=8,'seq_2'=4,'ch'=4] {'seq_0','seq_1','seq_2','ch'}, dimensions={0} | all-to-all | bytes 1441792 | tf_op jit(solution)/shard_map/all_to_all | solution.py:324
  111.0 1.0 reshape.19
  112.0 0.1 copy.20
  112.1 1.1 unpack.1
Async XLA Ops:
  0.6 0.9 copy-start
  1.5 0.9 copy-start.1
  2.4 0.9 copy-start.2
  3.3 0.9 copy-start.3
  4.3 0.9 copy-start.4
  5.2 0.8 copy-start.5

commit v3 on v2

--- a/solution.py
+++ b/solution.py
@@ -15,57 +15,61 @@
 OWN = 8
 GROUPS = 4
 PIECE = LANES // GROUPS
-WIDTH = 11 * LANES
+WIDTH = 6 * LANES
 MIB = 1024 * 1024
 
 f32 = jnp.float32
 bf16 = jnp.bfloat16
 
 
-def pack_kernel(q_ref, k_ref, v_ref, c_ref, h_ref, w_ref, out_ref, weight_ref):
-    half = out_ref.shape[0]
-    rows = [ref[...].astype(f32) for ref in (q_ref, k_ref, v_ref, c_ref)]
-    taps = h_ref[...].astype(f32)
-    wide = 2 * half
-    rows.append(jnp.concatenate([taps[:, g * wide : (g + 1) * wide] for g in range(GROUPS)], axis=0))
-    for index, value in enumerate(rows):
-        turned = value.T.astype(bf16)
-        for e in range(2):
-            column = (2 * index + e) * LANES
-            out_ref[:, column : column + LANES] = turned[e * half : (e + 1) * half]
+def pack_kernel(*refs):
+    sources, out_ref, copies = refs[:6], refs[6], refs[7:13]
+    weight_ref, sems = refs[13:]
+    moves = [
+        pltpu.make_async_copy(source, copy, sems.at[index])
+        for index, (source, copy) in enumerate(zip(sources, copies))
+    ]
+    for move in moves:
+        move.start()
+    pairs = (out_ref.shape[0], 2, LANES)
+    wide = out_ref.shape[0] * 2
+
+    def put(index, rows):
+        out_ref[:, :, index * LANES : (index + 1) * LANES] = rows.T.astype(bf16).reshape(pairs)
+
     weight_ref[...] = jnp.zeros_like(weight_ref)
+    for index in range(4):
+        moves[index].wait()
+        put(index, copies[index][...].astype(f32))
+    moves[4].wait()
+    taps = copies[4][...].astype(f32)
+    put(4, jnp.concatenate([taps[:, g * wide : (g + 1) * wide] for g in range(GROUPS)], axis=0))
+    moves[5].wait()
     for index in range(3):
-        weight = w_ref[index]
+        weight = copies[5][index]
         coarse = weight.astype(bf16).astype(f32)
-        for e in range(2):
-            part = slice(e * half, (e + 1) * half)
-            row = 64 * e + TAPS * index
-            weight_ref[row : row + TAPS, :] = coarse[:, part]
-            weight_ref[row + 32 : row + 32 + TAPS, :] = (weight - coarse)[:, part]
-    out_ref[:, 10 * LANES :] = weight_ref[...].T.astype(bf16)
+        row = TAPS * index
+        weight_ref[row : row + TAPS, :] = coarse
+        weight_ref[row + 32 : row + 32 + TAPS, :] = weight - coarse
+    put(5, weight_ref[...])
 
 
 def unpack_kernel(in_ref, mixed_ref, qg_ref, kg_ref, vg_ref, fg_ref, wg_ref):
-    half = in_ref.shape[0]
-
-    def turned(index, e):
-        column = (2 * index + e) * LANES
-        return in_ref[:, column : column + LANES].astype(f32).T
-
-    for e in range(2):
-        part = slice(e * half, (e + 1) * half)
-        for index, ref in enumerate((mixed_ref, qg_ref, kg_ref, vg_ref)):
-            ref[:, part] = turned(index, e).astype(bf16)
-        taps_grad = turned(4, e)
-        for g in range(GROUPS):
-            column = g * 2 * half + e * half
-            fg_ref[:, column : column + half] = taps_grad[g * PIECE : (g + 1) * PIECE]
-    sums = in_ref[:, 10 * LANES :].astype(f32).T
-    for e in range(2):
-        part = slice(e * half, (e + 1) * half)
-        total = sums[64 * e : 64 * e + 24] + sums[64 * e + 32 : 64 * e + 56]
-        for index in range(3):
-            wg_ref[index, :, part] = total[TAPS * index : TAPS * (index + 1)]
+    wide = in_ref.shape[0] * 2
+
+    def turned(index):
+        rows = in_ref[:, :, index * LANES : (index + 1) * LANES].reshape(wide, LANES)
+        return rows.astype(f32).T
+
+    for index, ref in enumerate((mixed_ref, qg_ref, kg_ref, vg_ref)):
+        ref[...] = turned(index).astype(bf16)
+    taps_grad = turned(4)
+    for g in range(GROUPS):
+        fg_ref[:, g * wide : (g + 1) * wide] = taps_grad[g * PIECE : (g + 1) * PIECE]
+    sums = turned(5)
+    total = sums[0:24] + sums[32:56]
+    for index in range(3):
+        wg_ref[index] = total[TAPS * index : TAPS * (index + 1)]
 
 
 def owner_kernel(
@@ -87,8 +91,7 @@
 ):
     lane = lax.broadcasted_iota(jnp.int32, (OWN, LANES), 1)
     row = lax.broadcasted_iota(jnp.int32, (OWN, LANES), 0)
-    first_half = row < GROUPS
-    group = row % GROUPS
+    group = row // 2
     piece = lane // PIECE
     flip_row = lax.broadcasted_iota(jnp.int32, (LANES, LANES), 0)
     flip_col = lax.broadcasted_iota(jnp.int32, (LANES, LANES), 1)
@@ -96,48 +99,36 @@
     zero = jnp.zeros((OWN, LANES), f32)
     steps = blocks // 4
 
-    def half_turn(value):
-        return pltpu.roll(value, GROUPS, 0)
-
-    def regroup(one, two):
-        return (
-            jnp.where(first_half, one, half_turn(two)),
-            jnp.where(first_half, half_turn(one), two),
-        )
-
     def swap_pieces(value):
         result = value
         for k in range(1, GROUPS):
-            moved = pltpu.roll(value, PIECE * k, 1)
-            up = pltpu.roll(moved, OWN - k, 0)
-            down = pltpu.roll(moved, GROUPS - k, 0)
-            taken = jnp.where(group + k < GROUPS, up, down)
-            result = jnp.where(piece == (group + k) % GROUPS, taken, result)
+            moved = pltpu.roll(pltpu.roll(value, PIECE * k, 1), OWN - 2 * k, 0)
+            result = jnp.where(piece == (group + k) % GROUPS, moved, result)
         return result
 
     def block_rows(s):
         return pl.ds(pl.multiple_of(s * OWN, OWN), OWN)
 
-    weights = in_ref[0:OWN, 10 * LANES :].astype(f32)
-    weights = jnp.where(first_half, weights, pltpu.roll(weights, 64, 1))
+    def taken(step, index):
+        rows = in_ref[pl.ds(step * 16, 16), :, index * LANES : (index + 1) * LANES]
+        return rows.reshape(4 * OWN, LANES).astype(f32)
+
+    weights = taken(0, 5)[:OWN]
     weights = weights + pltpu.roll(weights, LANES - 32, 1)
     for index in range(3 * TAPS):
         w_ref[index] = jnp.broadcast_to(weights[:, index : index + 1], (OWN, LANES))
 
     @pl.loop(0, steps)
     def _(step):
-        rows = pl.ds(pl.multiple_of(step * 16, 16), 16)
         for index in range(5):
-            one = in_ref[rows, 2 * index * LANES : (2 * index + 1) * LANES].astype(f32)
-            two = in_ref[rows, (2 * index + 1) * LANES : (2 * index + 2) * LANES].astype(f32)
-            for part in range(2):
-                pair = regroup(one[part * OWN : (part + 1) * OWN], two[part * OWN : (part + 1) * OWN])
-                for which, value in enumerate(pair):
-                    s = step * 4 + part * 2 + which
-                    if index < 4:
-                        raw_ref[index, s] = value
-                    else:
-                        tap_ref[block_rows(s), :] = swap_pieces(value)
+            values = taken(step, index)
+            for which in range(4):
+                s = step * 4 + which
+                value = values[which * OWN : (which + 1) * OWN]
+                if index < 4:
+                    raw_ref[index, s] = value
+                else:
+                    tap_ref[block_rows(s), :] = swap_pieces(value)
 
     for index in range(3):
 
@@ -174,16 +165,16 @@
     causal = flip_col >= flip_row
 
     def long_conv(r, toeplitz_ref, operand_refs):
-        before = jnp.zeros((LANES, LANES), f32)
+        before = jnp.zeros((LANES, LANES), bf16)
         totals = [[None] * (blocks // 16) for _ in operand_refs]
         for pair in range(blocks // 2):
             tiles = []
             for d in (2 * pair, 2 * pair + 1):
-                line = toeplitz_ref[r, blocks + d : blocks + d + 1, :]
+                line = toeplitz_ref[r, blocks + d : blocks + d + 1, :].astype(bf16)
                 turned = pltpu.roll(
                     jnp.broadcast_to(line, (LANES, LANES)), 0, 1, stride=1, stride_axis=0
                 )
-                tiles.append(jnp.where(causal, turned, before).astype(bf16))
+                tiles.append(jnp.where(causal, turned, before))
                 before = turned
             right = jnp.concatenate(tiles, axis=0)
             first = (2 * pair) // 16
@@ -217,11 +208,8 @@
     gate_ref[...] = jnp.dot(tap_ref[...].astype(bf16), flip, preferred_element_type=f32)
 
     def put(step, index, values):
-        ones, twos = zip(regroup(values[0], values[1]), regroup(values[2], values[3]))
-        rows = pl.ds(pl.multiple_of(step * 16, 16), 16)
-        for e, halves in enumerate((ones, twos)):
-            column = (2 * index + e) * LANES
-            out_ref[rows, column : column + LANES] = jnp.concatenate(halves, axis=0).astype(bf16)
+        rows = jnp.concatenate(values, axis=0).astype(bf16).reshape(16, 2, LANES)
+        out_ref[pl.ds(step * 16, 16), :, index * LANES : (index + 1) * LANES] = rows
 
     def back_block(s):
         return block_rows(blocks - 1 - s)
@@ -274,14 +262,11 @@
         coarse = total.astype(bf16).astype(f32)
         high = jnp.where(lane == index, coarse, high)
         low = jnp.where(lane == index + 32, total - coarse, low)
-    both = high + low
-    both = jnp.where(lane < 64, both, pltpu.roll(half_turn(both), 64, 1))
-    both = jnp.where(first_half, both, half_turn(both))
-    both = jnp.concatenate([both, both], axis=0).astype(bf16)
+    both = [high + low] * 4
 
     @pl.loop(0, steps)
     def _(step):
-        out_ref[pl.ds(pl.multiple_of(step * 16, 16), 16), 10 * LANES :] = both
+        put(step, 5, both)
 
 
 def on_device(query_raw, key_raw, value_raw, featurizer, filter_taps, cotangent):
@@ -290,15 +275,18 @@
     devices = lax.axis_size(SEQ_CH)
     small = pltpu.CompilerParams(vmem_limit_bytes=12 * MIB)
     large = pltpu.CompilerParams(vmem_limit_bytes=20 * MIB)
-    sent = jax.ShapeDtypeStruct((devices, WIDTH), bf16)
+    sent = jax.ShapeDtypeStruct((devices, 2, WIDTH), bf16)
+    sources = (query_raw, key_raw, value_raw, cotangent, filter_taps, featurizer)
 
     packed = pl.pallas_call(
         pack_kernel,
+        in_specs=[pl.BlockSpec(memory_space=pltpu.MemorySpace.HBM)] * len(sources),
         out_shape=sent,
-        scratch_shapes=[pltpu.VMEM((LANES, devices), f32)],
-        compiler_params=small,
+        scratch_shapes=[pltpu.VMEM(source.shape, source.dtype) for source in sources]
+        + [pltpu.VMEM((LANES, channels), f32), pltpu.SemaphoreType.DMA((len(sources),))],
+        compiler_params=pltpu.CompilerParams(vmem_limit_bytes=60 * MIB),
         name="pack",
-    )(query_raw, key_raw, value_raw, cotangent, filter_taps, featurizer)
+    )(*sources)
     received = lax.all_to_all(packed, SEQ_CH, split_axis=0, concat_axis=0, tiled=True)
 
     flat = pltpu.VMEM((blocks * OWN, LANES), f32)

time: 113 us -> 104 us (0.920)
  local copies, waits for them, and re-layouts: 9.48 us -> 0 us
  Pallas kernels: 28 us -> 30.3 us
  other arithmetic: 2.3 us -> 0 us
    unnamed x18 -> x0, local copies, waits for them, and re-layouts: 8.97 us -> none
    pallas_call x1, Pallas kernels: 0.27 us -> 2.75 us  [on_device(): pl.pallas_call(pack_kernel, in_specs=[pl.BlockSpec(memory_space=pltpu.Mem...]
    all_to_all x2 -> x0, other arithmetic: 2.3 us -> none  [the longest x1 1.15 us: on_device(): lax.all_to_all(outgoing, SEQ_CH, split_axis=0, concat_axis=0, tiled=True)]
where the time goes in v3:
time: 104 us
  blocking collectives  72.9 us (70%)
  Pallas kernels  30.3 us (29%)
    all_to_all x1, blocking collectives, on_device(): lax.all_to_all(packed, SEQ_CH, split_axis=0, concat_axis=0, tiled=True)  41.1 us
    all_to_all x1, blocking collectives, on_device(): lax.all_to_all(outgoing, SEQ_CH, split_axis=0, concat_axis=0, tiled=True)  31.8 us
    pallas_call x1, Pallas kernels, on_device(): pl.pallas_call(functools.partial(owner_kernel, blocks=blocks, scale=(bloc...  26.4 us
    pallas_call x1, Pallas kernels, on_device(): pl.pallas_call(pack_kernel, in_specs=[pl.BlockSpec(memory_space=pltpu.Mem...  2.75 us

profile of v3, /device:TPU:1, one launch (start us, length us, event | category | flops | bytes accessed | tf_op | source)
XLA Modules:
  0.0 103.9 jit_solution(9255641736417678946)
XLA Ops:
  0.6 2.7 %pack.1 = bf16[256,2,768]{2,1,0:T(2,128)(2,1)} custom-call(bf16[128,512]{1,0:T(8,128)(2,1)} %refs_0_.1, bf16[128,512]{1,0:T(8,128)(2,1)} %refs_1_.1, bf16[128,512]{1,0:T(8,128)(2,1)} %refs_2_.1, bf16[128,512]{1,0:T(8,128)(2,1)} %refs_3_.1, bf16[32,2048]{1,0:T(8,128)(2,1)} %refs_4_.1, f32[3,7,512]{2,1,0:T(8,128)} %refs_5_.1), custom_call_target="tpu_custom_call" | custom-call | tf_op jit(solution)/shard_map/pack/pallas_call | solution.py:281
  3.4 41.1 %all_to_all.10.in_ref = bf16[256,2,768]{2,1,0:T(2,128)(2,1)S(1)} all-to-all(bf16[256,2,768]{2,1,0:T(2,128)(2,1)} %pack.1), channel_id=1, replica_groups=mesh['seq_0'=2,'seq_1'=8,'seq_2'=4,'ch'=4] {'seq_0','seq_1','seq_2','ch'}, dimensions={0} | all-to-all | bytes 1572864 | tf_op jit(solution)/shard_map/all_to_all | solution.py:290
  44.5 26.4 %owner.1 = bf16[256,2,768]{2,1,0:T(2,128)(2,1)S(1)} custom-call(bf16[256,2,768]{2,1,0:T(2,128)(2,1)S(1)} %all_to_all.10.in_ref), custom_call_target="tpu_custom_call" | custom-call | tf_op jit(solution)/shard_map/owner/pallas_call | solution.py:294
  70.9 31.8 %all_to_all.11.in_ref = bf16[256,2,768]{2,1,0:T(2,128)(2,1)S(1)} all-to-all(bf16[256,2,768]{2,1,0:T(2,128)(2,1)S(1)} %owner.1), channel_id=1, replica_groups=mesh['seq_0'=2,'seq_1'=8,'seq_2'=4,'ch'=4] {'seq_0','seq_1','seq_2','ch'}, dimensions={0} | all-to-all | bytes 1572864 | tf_op jit(solution)/shard_map/all_to_all | solution.py:312
  102.6 1.2 %unpack.1 = (bf16[128,512]{1,0:T(8,128)(2,1)}, bf16[128,512]{1,0:T(8,128)(2,1)}, bf16[128,512]{1,0:T(8,128)(2,1)}, bf16[128,512]{1,0:T(8,128)(2,1)}, f32[32,2048]{1,0:T(8,128)}, /*index=5*/f32[3,7,512]{2,1,0:T(8,128)}) custom-call(bf16[256,2,768]{2,1,0:T(2,128)(2,1)S(1)} %all_to_all.11.in_ref), custom_call_target="tpu_custom_call" | custom-call | tf_op jit(solution)/shard_map/unpack/pallas_call | solution.py:315

commit v4 on v3

--- a/solution.py
+++ b/solution.py
@@ -15,6 +15,7 @@
 OWN = 8
 GROUPS = 4
 PIECE = LANES // GROUPS
+DEPTH = 12
 WIDTH = 6 * LANES
 MIB = 1024 * 1024
 
@@ -82,9 +83,11 @@
     gate_ref,
     tap_ref,
     xm_ref,
-    xg_ref,
     xh_ref,
     res_ref,
+    left_ref,
+    lhs_ref,
+    acc_ref,
     *,
     blocks,
     scale,
@@ -106,6 +109,12 @@
             result = jnp.where(piece == (group + k) % GROUPS, moved, result)
         return result
 
+    def summed(terms):
+        while len(terms) > 1:
+            pairs = [one + two for one, two in zip(terms[::2], terms[1::2])]
+            terms = pairs + terms[len(pairs) * 2 :]
+        return terms[0]
+
     def block_rows(s):
         return pl.ds(pl.multiple_of(s * OWN, OWN), OWN)
 
@@ -118,7 +127,7 @@
     for index in range(3 * TAPS):
         w_ref[index] = jnp.broadcast_to(weights[:, index : index + 1], (OWN, LANES))
 
-    @pl.loop(0, steps)
+    @pl.loop(0, steps, unroll=16)
     def _(step):
         for index in range(5):
             values = taken(step, index)
@@ -133,14 +142,15 @@
     for index in range(3):
 
         def forward(step, kept, index=index):
-            for which in range(4):
-                s = step * 4 + which
+            for which in range(64):
+                s = step * 64 + which
                 block = raw_ref[index, s]
                 rolled = tuple(pltpu.roll(block, j, 1) for j in range(1, TAPS))
-                total = w_ref[index * TAPS] * block
+                terms = [w_ref[index * TAPS] * block]
                 for j in range(1, TAPS):
                     shifted = jnp.where(lane >= j, rolled[j - 1], kept[j - 1])
-                    total = total + w_ref[index * TAPS + j] * shifted
+                    terms.append(w_ref[index * TAPS + j] * shifted)
+                total = summed(terms)
                 kept = rolled
                 feat_ref[index, s] = total
                 if index == 0:
@@ -149,60 +159,90 @@
                     mix_ref[block_rows(s), :] = (feat_ref[1, s] * total).astype(bf16).astype(f32)
             return kept
 
-        lax.fori_loop(0, steps, forward, (zero,) * (TAPS - 1))
+        lax.fori_loop(0, blocks // 64, forward, (zero,) * (TAPS - 1))
 
     res_ref[...] = jnp.dot(gate_ref[...].astype(bf16), flip, preferred_element_type=f32)
 
-    @pl.loop(0, blocks)
-    def _(s):
-        gate_ref[block_rows(s), :] = res_ref[block_rows(blocks - 1 - s), :]
+    for b in range(GROUPS):
+        for o in range(2):
+            left_ref[o, b, : DEPTH * OWN, :] = jnp.zeros((DEPTH * OWN, LANES), f32)
+
+    def lay(step, carry):
+        carry = list(carry)
+        for which in range(4):
+            s = step * 4 + which
+            sources = (mix_ref[block_rows(s), :], res_ref[block_rows(blocks - 1 - s), :])
+            rows = pl.ds(pl.multiple_of((s + DEPTH) * OWN, OWN), OWN)
+            for o, value in enumerate(sources):
+                turns = (value,) + tuple(pltpu.roll(value, PIECE * k, 1) for k in range(1, GROUPS))
+                history = (turns,) + carry[o]
+                for b in range(GROUPS):
+                    laid = history[0][-b % GROUPS]
+                    for p in range(1, GROUPS):
+                        laid = jnp.where(piece == p, history[p][(p - b) % GROUPS], laid)
+                    left_ref[o, b, rows, :] = laid
+                carry[o] = history[: GROUPS - 1]
+        return tuple(carry)
+
+    blank = ((zero,) * GROUPS,) * (GROUPS - 1)
+    lax.fori_loop(0, steps, lay, (blank, blank), unroll=16)
 
     for r in range(OWN):
-        for source, target in ((mix_ref, xm_ref), (gate_ref, xg_ref), (tap_ref, xh_ref)):
-            target[r, :blocks, :] = jnp.zeros((blocks, LANES), f32)
-            target[r, blocks:, :] = source[pl.ds(r, blocks, stride=OWN), :]
-
-    causal = flip_col >= flip_row
-
-    def long_conv(r, toeplitz_ref, operand_refs):
-        before = jnp.zeros((LANES, LANES), bf16)
-        totals = [[None] * (blocks // 16) for _ in operand_refs]
-        for pair in range(blocks // 2):
+        for source, target in ((mix_ref, xm_ref), (tap_ref, xh_ref)):
+            target[r] = source[pl.ds(r, blocks, stride=OWN), :]
+
+    tile_row = lax.broadcasted_iota(jnp.int32, (PIECE, LANES), 0)
+    tile_col = lax.broadcasted_iota(jnp.int32, (PIECE, LANES), 1)
+    causal = tile_col >= tile_row
+    full_row = lax.broadcasted_iota(jnp.int32, (blocks, LANES), 0)
+    full_col = lax.broadcasted_iota(jnp.int32, (blocks, LANES), 1)
+    reach = 4 * GROUPS
+
+    def long_conv(r, signal_ref, operands):
+        before = jnp.zeros((PIECE, LANES), f32)
+        for part in range(blocks // reach):
             tiles = []
-            for d in (2 * pair, 2 * pair + 1):
-                line = toeplitz_ref[r, blocks + d : blocks + d + 1, :].astype(bf16)
-                turned = pltpu.roll(
-                    jnp.broadcast_to(line, (LANES, LANES)), 0, 1, stride=1, stride_axis=0
-                )
-                tiles.append(jnp.where(causal, turned, before))
+            for mu in range(part * reach, (part + 1) * reach):
+                line = jnp.broadcast_to(signal_ref[r, mu : mu + 1, :], (PIECE, LANES))
+                turned = pltpu.roll(line, 0, 1, stride=1, stride_axis=0)
+                tiles.append(jnp.where(causal, turned, before).astype(bf16))
                 before = turned
             right = jnp.concatenate(tiles, axis=0)
-            first = (2 * pair) // 16
-            for o, operand_ref in enumerate(operand_refs):
-                left = jnp.concatenate(
-                    [
-                        operand_ref[r, blocks - d + 16 * first : 2 * blocks - d, :].astype(bf16)
-                        for d in (2 * pair, 2 * pair + 1)
-                    ],
-                    axis=1,
-                )
+            start = part * reach
+            height = blocks - start
+            for o in operands:
+                left = lhs_ref[o, :, :height, :].reshape(GROUPS * height, reach * PIECE)
                 product = jnp.dot(left, right, preferred_element_type=f32)
-                for part in range(first, blocks // 16):
-                    added = product[16 * (part - first) : 16 * (part - first + 1)]
-                    old = totals[o][part]
-                    totals[o][part] = added if old is None else old + added
-        return [jnp.concatenate(parts, axis=0) for parts in totals]
-
-    @pl.loop(0, OWN)
+                product = product.reshape(GROUPS, height, LANES)
+                if part == 0:
+                    acc_ref[o] = product
+                else:
+                    acc_ref[o, :, start:, :] += product
+
+    def gathered(o):
+        total = acc_ref[o, 0]
+        wrapped = jnp.zeros((blocks, LANES), f32)
+        for b in range(1, GROUPS):
+            moved = pltpu.roll(acc_ref[o, b], PIECE * b, 1)
+            inside = full_col >= PIECE * b
+            total = total + jnp.where(inside, moved, 0.0)
+            wrapped = wrapped + jnp.where(inside, 0.0, moved)
+        return total + jnp.where(full_row > 0, pltpu.roll(wrapped, 1, 0), 0.0)
+
+    @pl.loop(0, OWN, unroll=4)
     def _(r):
-        (taps_sum,) = long_conv(r, xm_ref, (xg_ref,))
-        tap_ref[pl.ds(r, blocks, stride=OWN), :] = taps_sum * scale
-
-    @pl.loop(0, OWN)
-    def _(r):
-        conv, mix_grad = long_conv(r, xh_ref, (xm_ref, xg_ref))
-        mix_ref[pl.ds(r, blocks, stride=OWN), :] = conv
-        gate_ref[pl.ds(r, blocks, stride=OWN), :] = mix_grad
+        for o in range(2):
+            for b in range(GROUPS):
+                for depth in range(GROUPS):
+                    rows = pl.ds((DEPTH - GROUPS * depth) * OWN + r, blocks, stride=OWN)
+                    lanes = slice(depth * LANES, (depth + 1) * LANES)
+                    lhs_ref[o, b, :, lanes] = left_ref[o, b, rows, :].astype(bf16)
+        here = pl.ds(r, blocks, stride=OWN)
+        long_conv(r, xm_ref, (1,))
+        tap_ref[here, :] = gathered(1) * scale
+        long_conv(r, xh_ref, (0, 1))
+        mix_ref[here, :] = gathered(0)
+        gate_ref[here, :] = gathered(1)
 
     res_ref[...] = jnp.dot(gate_ref[...].astype(bf16), flip, preferred_element_type=f32)
     gate_ref[...] = jnp.dot(tap_ref[...].astype(bf16), flip, preferred_element_type=f32)
@@ -214,7 +254,7 @@
     def back_block(s):
         return block_rows(blocks - 1 - s)
 
-    @pl.loop(0, steps)
+    @pl.loop(0, steps, unroll=16)
     def _(step):
         mixed, taps_grad = [], []
         for which in range(4):
@@ -230,29 +270,32 @@
     for index in range(3):
 
         def backward(count, carry, index=index):
-            step = steps - 1 - count
             kept, sums = carry
-            grads = [None] * 4
-            for which in (3, 2, 1, 0):
-                s = step * 4 + which
-                if index == 0:
-                    grad = raw_ref[3, s] * mix_ref[block_rows(s), :]
-                else:
-                    grad = res_ref[back_block(s), :] * feat_ref[3 - index, s]
-                raw = raw_ref[index, s]
-                rolled = tuple(pltpu.roll(grad, LANES - j, 1) for j in range(1, TAPS))
-                total = w_ref[index * TAPS] * grad
-                new_sums = [sums[0] + raw * grad]
-                for j in range(1, TAPS):
-                    shifted = jnp.where(lane < LANES - j, rolled[j - 1], kept[j - 1])
-                    total = total + w_ref[index * TAPS + j] * shifted
-                    new_sums.append(sums[j] + raw * shifted)
-                kept, sums = rolled, tuple(new_sums)
-                grads[which] = total
-            put(step, index + 1, grads)
+            for sub in reversed(range(64 // 4)):
+                step = (blocks // 64 - 1 - count) * (64 // 4) + sub
+                grads = [None] * 4
+                for which in (3, 2, 1, 0):
+                    s = step * 4 + which
+                    if index == 0:
+                        grad = raw_ref[3, s] * mix_ref[block_rows(s), :]
+                    else:
+                        grad = res_ref[back_block(s), :] * feat_ref[3 - index, s]
+                    raw = raw_ref[index, s]
+                    rolled = tuple(pltpu.roll(grad, LANES - j, 1) for j in range(1, TAPS))
+                    terms = [w_ref[index * TAPS] * grad]
+                    new_sums = [sums[0] + raw * grad]
+                    for j in range(1, TAPS):
+                        shifted = jnp.where(lane < LANES - j, rolled[j - 1], kept[j - 1])
+                        terms.append(w_ref[index * TAPS + j] * shifted)
+                        new_sums.append(sums[j] + raw * shifted)
+                    kept, sums = rolled, tuple(new_sums)
+                    grads[which] = summed(terms)
+                put(step, index + 1, grads)
             return kept, sums
 
-        _, sums = lax.fori_loop(0, steps, backward, ((zero,) * (TAPS - 1), (zero,) * TAPS))
+        _, sums = lax.fori_loop(
+            0, blocks // 64, backward, ((zero,) * (TAPS - 1), (zero,) * TAPS)
+        )
         all_sums += sums
 
     high = zero
@@ -264,8 +307,7 @@
         low = jnp.where(lane == index + 32, total - coarse, low)
     both = [high + low] * 4
 
-    @pl.loop(0, steps)
-    def _(step):
+    for step in range(steps):
         put(step, 5, both)
 
 
@@ -290,7 +332,7 @@
     received = lax.all_to_all(packed, SEQ_CH, split_axis=0, concat_axis=0, tiled=True)
 
     flat = pltpu.VMEM((blocks * OWN, LANES), f32)
-    by_channel = pltpu.VMEM((OWN, 2 * blocks, LANES), f32)
+    by_channel = pltpu.VMEM((OWN, blocks, LANES), f32)
     outgoing = pl.pallas_call(
         functools.partial(owner_kernel, blocks=blocks, scale=(blocks * LANES) ** -0.5),
         out_shape=sent,
@@ -303,8 +345,10 @@
             flat,
             by_channel,
             by_channel,
-            by_channel,
             flat,
+            pltpu.VMEM((2, GROUPS, (blocks + DEPTH) * OWN, LANES), f32),
+            pltpu.VMEM((2, GROUPS, blocks, GROUPS * LANES), bf16),
+            pltpu.VMEM((2, GROUPS, blocks, LANES), f32),
         ],
         compiler_params=large,
         name="owner",

time: 104 us -> 87.7 us (0.84)
  Pallas kernels: 30.3 us -> 14 us
    pallas_call x1, Pallas kernels: 26.4 us -> 10 us  [on_device(): pl.pallas_call(functools.partial(owner_kernel, blocks=blocks, scale=(bloc...]
where the time goes in v4:
time: 87.7 us; the launch traced here: 87.6 us
  blocking collectives  72.9 us (83%)
  Pallas kernels  14 us (16%)
    all_to_all x1, blocking collectives, on_device(): lax.all_to_all(packed, SEQ_CH, split_axis=0, concat_axis=0, tiled=True)  41.1 us
    all_to_all x1, blocking collectives, on_device(): lax.all_to_all(outgoing, SEQ_CH, split_axis=0, concat_axis=0, tiled=True)  31.8 us
    pallas_call x1, Pallas kernels, on_device(): pl.pallas_call(functools.partial(owner_kernel, blocks=blocks, scale=(bloc...  10 us
    pallas_call x1, Pallas kernels, on_device(): pl.pallas_call(pack_kernel, in_specs=[pl.BlockSpec(memory_space=pltpu.Mem...  2.75 us

profile of v4, /device:TPU:1, one launch (start us, length us, event | category | flops | bytes accessed | tf_op | source)
XLA Modules:
  0.0 87.6 jit_solution(2278715273144610072)
XLA Ops:
  0.6 2.7 %pack.1 = bf16[256,2,768]{2,1,0:T(2,128)(2,1)} custom-call(bf16[128,512]{1,0:T(8,128)(2,1)} %refs_0_.1, bf16[128,512]{1,0:T(8,128)(2,1)} %refs_1_.1, bf16[128,512]{1,0:T(8,128)(2,1)} %refs_2_.1, bf16[128,512]{1,0:T(8,128)(2,1)} %refs_3_.1, bf16[32,2048]{1,0:T(8,128)(2,1)} %refs_4_.1, f32[3,7,512]{2,1,0:T(8,128)} %refs_5_.1), custom_call_target="tpu_custom_call" | custom-call | tf_op jit(solution)/shard_map/pack/pallas_call | solution.py:323
  3.4 41.1 %all_to_all.10.in_ref = bf16[256,2,768]{2,1,0:T(2,128)(2,1)S(1)} all-to-all(bf16[256,2,768]{2,1,0:T(2,128)(2,1)} %pack.1), channel_id=1, replica_groups=mesh['seq_0'=2,'seq_1'=8,'seq_2'=4,'ch'=4] {'seq_0','seq_1','seq_2','ch'}, dimensions={0} | all-to-all | bytes 1572864 | tf_op jit(solution)/shard_map/all_to_all | solution.py:332
  44.5 10.0 %owner.1 = bf16[256,2,768]{2,1,0:T(2,128)(2,1)S(1)} custom-call(bf16[256,2,768]{2,1,0:T(2,128)(2,1)S(1)} %all_to_all.10.in_ref), custom_call_target="tpu_custom_call" | custom-call | tf_op jit(solution)/shard_map/owner/pallas_call | solution.py:336
  54.5 31.8 %all_to_all.11.in_ref = bf16[256,2,768]{2,1,0:T(2,128)(2,1)S(1)} all-to-all(bf16[256,2,768]{2,1,0:T(2,128)(2,1)S(1)} %owner.1), channel_id=1, replica_groups=mesh['seq_0'=2,'seq_1'=8,'seq_2'=4,'ch'=4] {'seq_0','seq_1','seq_2','ch'}, dimensions={0} | all-to-all | bytes 1572864 | tf_op jit(solution)/shard_map/all_to_all | solution.py:356
  86.3 1.2 %unpack.1 = (bf16[128,512]{1,0:T(8,128)(2,1)}, bf16[128,512]{1,0:T(8,128)(2,1)}, bf16[128,512]{1,0:T(8,128)(2,1)}, bf16[128,512]{1,0:T(8,128)(2,1)}, f32[32,2048]{1,0:T(8,128)}, /*index=5*/f32[3,7,512]{2,1,0:T(8,128)}) custom-call(bf16[256,2,768]{2,1,0:T(2,128)(2,1)S(1)} %all_to_all.11.in_ref), custom_call_target="tpu_custom_call" | custom-call | tf_op jit(solution)/shard_map/unpack/pallas_call | solution.py:359

commit v5 on v4

--- a/solution.py
+++ b/solution.py
@@ -16,7 +16,6 @@
 GROUPS = 4
 PIECE = LANES // GROUPS
 DEPTH = 12
-WIDTH = 6 * LANES
 MIB = 1024 * 1024
 
 f32 = jnp.float32
@@ -24,8 +23,7 @@
 
 
 def pack_kernel(*refs):
-    sources, out_ref, copies = refs[:6], refs[6], refs[7:13]
-    weight_ref, sems = refs[13:]
+    sources, out_ref, copies, sems = refs[:5], refs[5], refs[6:11], refs[11]
     moves = [
         pltpu.make_async_copy(source, copy, sems.at[index])
         for index, (source, copy) in enumerate(zip(sources, copies))
@@ -38,21 +36,12 @@
     def put(index, rows):
         out_ref[:, :, index * LANES : (index + 1) * LANES] = rows.T.astype(bf16).reshape(pairs)
 
-    weight_ref[...] = jnp.zeros_like(weight_ref)
     for index in range(4):
         moves[index].wait()
         put(index, copies[index][...].astype(f32))
     moves[4].wait()
     taps = copies[4][...].astype(f32)
     put(4, jnp.concatenate([taps[:, g * wide : (g + 1) * wide] for g in range(GROUPS)], axis=0))
-    moves[5].wait()
-    for index in range(3):
-        weight = copies[5][index]
-        coarse = weight.astype(bf16).astype(f32)
-        row = TAPS * index
-        weight_ref[row : row + TAPS, :] = coarse
-        weight_ref[row + 32 : row + 32 + TAPS, :] = weight - coarse
-    put(5, weight_ref[...])
 
 
 def unpack_kernel(in_ref, mixed_ref, qg_ref, kg_ref, vg_ref, fg_ref, wg_ref):
@@ -75,6 +64,7 @@
 
 def owner_kernel(
     in_ref,
+    own_ref,
     out_ref,
     w_ref,
     raw_ref,
@@ -122,10 +112,8 @@
         rows = in_ref[pl.ds(step * 16, 16), :, index * LANES : (index + 1) * LANES]
         return rows.reshape(4 * OWN, LANES).astype(f32)
 
-    weights = taken(0, 5)[:OWN]
-    weights = weights + pltpu.roll(weights, LANES - 32, 1)
     for index in range(3 * TAPS):
-        w_ref[index] = jnp.broadcast_to(weights[:, index : index + 1], (OWN, LANES))
+        w_ref[index] = jnp.broadcast_to(own_ref[:, index : index + 1], (OWN, LANES))
 
     @pl.loop(0, steps, unroll=16)
     def _(step):
@@ -198,21 +186,30 @@
     full_col = lax.broadcasted_iota(jnp.int32, (blocks, LANES), 1)
     reach = 4 * GROUPS
 
-    def long_conv(r, signal_ref, operands):
-        before = jnp.zeros((PIECE, LANES), f32)
+    def toeplitz(r, signal_ref, part, before):
+        tiles = []
+        for mu in range(part * reach, (part + 1) * reach):
+            line = jnp.broadcast_to(signal_ref[r, mu : mu + 1, :], (PIECE, LANES))
+            turned = pltpu.roll(line, 0, 1, stride=1, stride_axis=0)
+            tiles.append(jnp.where(causal, turned, before).astype(bf16))
+            before = turned
+        return jnp.concatenate(tiles, axis=0), before
+
+    def long_convs(r):
+        before_taps = before_mix = jnp.zeros((PIECE, LANES), f32)
         for part in range(blocks // reach):
-            tiles = []
-            for mu in range(part * reach, (part + 1) * reach):
-                line = jnp.broadcast_to(signal_ref[r, mu : mu + 1, :], (PIECE, LANES))
-                turned = pltpu.roll(line, 0, 1, stride=1, stride_axis=0)
-                tiles.append(jnp.where(causal, turned, before).astype(bf16))
-                before = turned
-            right = jnp.concatenate(tiles, axis=0)
+            taps, before_taps = toeplitz(r, xh_ref, part, before_taps)
+            mix, before_mix = toeplitz(r, xm_ref, part, before_mix)
             start = part * reach
             height = blocks - start
-            for o in operands:
-                left = lhs_ref[o, :, :height, :].reshape(GROUPS * height, reach * PIECE)
-                product = jnp.dot(left, right, preferred_element_type=f32)
+            flat = (GROUPS * height, reach * PIECE)
+            one = jnp.dot(lhs_ref[0, :, :height, :].reshape(flat), taps, preferred_element_type=f32)
+            two = jnp.dot(
+                lhs_ref[1, :, :height, :].reshape(flat),
+                jnp.concatenate([taps, mix], axis=1),
+                preferred_element_type=f32,
+            )
+            for o, product in enumerate((one, two[:, :LANES], two[:, LANES:])):
                 product = product.reshape(GROUPS, height, LANES)
                 if part == 0:
                     acc_ref[o] = product
@@ -238,11 +235,10 @@
                     lanes = slice(depth * LANES, (depth + 1) * LANES)
                     lhs_ref[o, b, :, lanes] = left_ref[o, b, rows, :].astype(bf16)
         here = pl.ds(r, blocks, stride=OWN)
-        long_conv(r, xm_ref, (1,))
-        tap_ref[here, :] = gathered(1) * scale
-        long_conv(r, xh_ref, (0, 1))
+        long_convs(r)
         mix_ref[here, :] = gathered(0)
         gate_ref[here, :] = gathered(1)
+        tap_ref[here, :] = gathered(2) * scale
 
     res_ref[...] = jnp.dot(gate_ref[...].astype(bf16), flip, preferred_element_type=f32)
     gate_ref[...] = jnp.dot(tap_ref[...].astype(bf16), flip, preferred_element_type=f32)
@@ -317,25 +313,29 @@
     devices = lax.axis_size(SEQ_CH)
     small = pltpu.CompilerParams(vmem_limit_bytes=12 * MIB)
     large = pltpu.CompilerParams(vmem_limit_bytes=20 * MIB)
-    sent = jax.ShapeDtypeStruct((devices, 2, WIDTH), bf16)
-    sources = (query_raw, key_raw, value_raw, cotangent, filter_taps, featurizer)
+    me = lax.axis_index(SEQ_CH)
+    sources = (query_raw, key_raw, value_raw, cotangent, filter_taps)
 
     packed = pl.pallas_call(
         pack_kernel,
         in_specs=[pl.BlockSpec(memory_space=pltpu.MemorySpace.HBM)] * len(sources),
-        out_shape=sent,
+        out_shape=jax.ShapeDtypeStruct((devices, 2, 5 * LANES), bf16),
         scratch_shapes=[pltpu.VMEM(source.shape, source.dtype) for source in sources]
-        + [pltpu.VMEM((LANES, channels), f32), pltpu.SemaphoreType.DMA((len(sources),))],
+        + [pltpu.SemaphoreType.DMA((len(sources),))],
         compiler_params=pltpu.CompilerParams(vmem_limit_bytes=60 * MIB),
         name="pack",
     )(*sources)
     received = lax.all_to_all(packed, SEQ_CH, split_axis=0, concat_axis=0, tiled=True)
 
+    weights = lax.all_gather(featurizer, "ch")
+    weights = lax.dynamic_slice(weights, (0, 0, 0, 2 * me), (GROUPS, 3, TAPS, 2))
+    weights = weights.transpose(0, 3, 1, 2).reshape(OWN, 3 * TAPS)
+
     flat = pltpu.VMEM((blocks * OWN, LANES), f32)
     by_channel = pltpu.VMEM((OWN, blocks, LANES), f32)
     outgoing = pl.pallas_call(
         functools.partial(owner_kernel, blocks=blocks, scale=(blocks * LANES) ** -0.5),
-        out_shape=sent,
+        out_shape=jax.ShapeDtypeStruct((devices, 2, 6 * LANES), bf16),
         scratch_shapes=[
             pltpu.VMEM((3 * TAPS, OWN, LANES), f32),
             pltpu.VMEM((4, blocks, OWN, LANES), f32),
@@ -348,11 +348,11 @@
             flat,
             pltpu.VMEM((2, GROUPS, (blocks + DEPTH) * OWN, LANES), f32),
             pltpu.VMEM((2, GROUPS, blocks, GROUPS * LANES), bf16),
-            pltpu.VMEM((2, GROUPS, blocks, LANES), f32),
+            pltpu.VMEM((3, GROUPS, blocks, LANES), f32),
         ],
         compiler_params=large,
         name="owner",
-    )(received)
+    )(received, weights)
     returned = lax.all_to_all(outgoing, SEQ_CH, split_axis=0, concat_axis=0, tiled=True)
 
     here = jax.ShapeDtypeStruct((tok_rows, channels), bf16)

time: 87.7 us -> 83.8 us (0.956)
  blocking collectives: 72.9 us -> 39.3 us
  starting transfers between devices: 0 us -> 15.7 us
  waiting for transfers between devices: 0 us -> 14.8 us
  Pallas kernels: 14 us -> 12.9 us
    all_to_all x1 -> x0, blocking collectives: 41.1 us -> none  [on_device(): lax.all_to_all(packed, SEQ_CH, split_axis=0, concat_axis=0, tiled=True)]
    all_to_all x0 -> x1, starting transfers between devices: none -> 15.7 us  [on_device(): lax.all_to_all(packed, SEQ_CH, split_axis=0, concat_axis=0, tiled=True)]
    all_to_all x0 -> x1, waiting for transfers between devices: none -> 14.8 us  [on_device(): lax.all_to_all(packed, SEQ_CH, split_axis=0, concat_axis=0, tiled=True)]
    all_gather x0 -> x1, blocking collectives: none -> 7.92 us  [on_device(): weights = lax.all_gather(featurizer, 'ch')]
    pallas_call x1, Pallas kernels: 10 us -> 9.09 us  [on_device(): pl.pallas_call(functools.partial(owner_kernel, blocks=blocks, scale=(bloc...]
  transfers between devices with their start and end apart: 0 -> 1, of which waited for: 0 -> 1; matrix products, arithmetic and copies ran while one was open for 0% -> 0% of each run, Pallas kernels for 0% -> 0%
where the time goes in v5:
time: 83.8 us; the launch traced here: 83.6 us
  blocking collectives  39.3 us (47%)
  starting transfers between devices  15.7 us (19%)
  waiting for transfers between devices  14.8 us (18%)
  Pallas kernels  12.9 us (15%)
    all_to_all x1, blocking collectives, on_device(): lax.all_to_all(outgoing, SEQ_CH, split_axis=0, concat_axis=0, tiled=True)  31.3 us
    all_to_all x1, starting transfers between devices, on_device(): lax.all_to_all(packed, SEQ_CH, split_axis=0, concat_axis=0, tiled=True)  15.7 us
    all_to_all x1, waiting for transfers between devices, on_device(): lax.all_to_all(packed, SEQ_CH, split_axis=0, concat_axis=0, tiled=True)  14.8 us
    pallas_call x1, Pallas kernels, on_device(): pl.pallas_call(functools.partial(owner_kernel, blocks=blocks, scale=(bloc...  9.09 us
    all_gather x1, blocking collectives, on_device(): weights = lax.all_gather(featurizer, 'ch')  7.92 us
    pallas_call x1, Pallas kernels, on_device(): pl.pallas_call(pack_kernel, in_specs=[pl.BlockSpec(memory_space=pltpu.Mem...  2.54 us
  transfers between devices with their start and end apart: 1, of which 1 were waited for; matrix products, arithmetic and copies ran while one was open for 0% of the time, Pallas kernels for 0%

profile of v5, /device:TPU:1, one launch (start us, length us, event | category | flops | bytes accessed | tf_op | source)
XLA Modules:
  0.0 83.6 jit_solution(8595097074358662388)
XLA Ops:
  0.6 2.5 %pack.1 = bf16[256,2,640]{2,1,0:T(2,128)(2,1)} custom-call(bf16[128,512]{1,0:T(8,128)(2,1)} %refs_0_.1, bf16[128,512]{1,0:T(8,128)(2,1)} %refs_1_.1, bf16[128,512]{1,0:T(8,128)(2,1)} %refs_2_.1, bf16[128,512]{1,0:T(8,128)(2,1)} %refs_3_.1, bf16[32,2048]{1,0:T(8,128)(2,1)} %refs_4_.1), custom_call_target="tpu_custom_call" | custom-call | tf_op jit(solution)/shard_map/pack/pallas_call | solution.py:319
  3.2 0.0 copy-start
  3.2 15.7 %all-to-all-start = ((bf16[256,2,640]{2,1,0:T(2,128)(2,1)}), bf16[256,2,640]{2,1,0:T(2,128)(2,1)S(1)}, u32[]{:S(2)}, u32[]{:S(2)}) async-start(bf16[256,2,640]{2,1,0:T(2,128)(2,1)} %pack.1), calls=%async_computation | async-start | bytes 1310720 | tf_op jit(solution)/shard_map/all_to_all | solution.py:328
  18.9 0.0 copy-done
  18.9 7.9 %all-gather = f32[12,7,512]{2,1,0:T(8,128)S(1)} all-gather(f32[3,7,512]{2,1,0:T(8,128)S(1)} %copy-done), channel_id=2, replica_groups=mesh['seq_0'=2,'seq_1'=8,'seq_2'=4,'ch'=4] {'ch'}, dimensions={0}, use_global_device_ids=true | all-gather | bytes 215040 | tf_op jit(solution)/shard_map/all_gather | solution.py:330
  26.8 0.1 constant_dynamic-slice_fusion
  26.9 0.2 copy.15
  27.1 0.1 reshape.15.own_ref
  27.1 14.8 %all-to-all-done.in_ref = bf16[256,2,640]{2,1,0:T(2,128)(2,1)S(1)} async-done(((bf16[256,2,640]{2,1,0:T(2,128)(2,1)}), bf16[256,2,640]{2,1,0:T(2,128)(2,1)S(1)}, u32[]{:S(2)}, u32[]{:S(2)}) %all-to-all-start) | async-done | bytes 655392 | tf_op jit(solution)/shard_map/all_to_all | solution.py:328
  41.9 9.1 %owner.1 = bf16[256,2,768]{2,1,0:T(2,128)(2,1)S(1)} custom-call(bf16[256,2,640]{2,1,0:T(2,128)(2,1)S(1)} %all-to-all-done.in_ref, f32[8,21]{1,0:T(8,128)S(1)} %reshape.15.own_ref), custom_call_target="tpu_custom_call" | custom-call | tf_op jit(solution)/shard_map/owner/pallas_call | solution.py:336
  51.0 31.3 %all_to_all.10.in_ref = bf16[256,2,768]{2,1,0:T(2,128)(2,1)S(1)} all-to-all(bf16[256,2,768]{2,1,0:T(2,128)(2,1)S(1)} %owner.1), channel_id=1, replica_groups=mesh['seq_0'=2,'seq_1'=8,'seq_2'=4,'ch'=4] {'seq_0','seq_1','seq_2','ch'}, dimensions={0} | all-to-all | bytes 1572864 | tf_op jit(solution)/shard_map/all_to_all | solution.py:356
  82.4 1.2 %unpack.1 = (bf16[128,512]{1,0:T(8,128)(2,1)}, bf16[128,512]{1,0:T(8,128)(2,1)}, bf16[128,512]{1,0:T(8,128)(2,1)}, bf16[128,512]{1,0:T(8,128)(2,1)}, f32[32,2048]{1,0:T(8,128)}, /*index=5*/f32[3,7,512]{2,1,0:T(8,128)}) custom-call(bf16[256,2,768]{2,1,0:T(2,128)(2,1)S(1)} %all_to_all.10.in_ref), custom_call_target="tpu_custom_call" | custom-call | tf_op jit(solution)/shard_map/unpack/pallas_call | solution.py:359
Async XLA Ops:
  3.2 15.7 %copy-start = (f32[3,7,512]{2,1,0:T(8,128)S(1)}, f32[3,7,512]{2,1,0:T(8,128)}, u32[]{:S(2)}) copy-start(f32[3,7,512]{2,1,0:T(8,128)} %param.9) | copy-start | bytes 129028
  3.2 38.8 %all-to-all-start = ((bf16[256,2,640]{2,1,0:T(2,128)(2,1)}), bf16[256,2,640]{2,1,0:T(2,128)(2,1)S(1)}, u32[]{:S(2)}, u32[]{:S(2)}) async-start(bf16[256,2,640]{2,1,0:T(2,128)(2,1)} %pack.1), calls=%async_computation | async-start | bytes 1310720 | tf_op jit(solution)/shard_map/all_to_all | solution.py:328

commit v6 on v5

--- a/solution.py
+++ b/solution.py
@@ -44,22 +44,85 @@
     put(4, jnp.concatenate([taps[:, g * wide : (g + 1) * wide] for g in range(GROUPS)], axis=0))
 
 
-def unpack_kernel(in_ref, mixed_ref, qg_ref, kg_ref, vg_ref, fg_ref, wg_ref):
+def feat_kernel(q_ref, k_ref, v_ref, w_ref, fq_ref, fk_ref, fv_ref, padded_ref):
+    rows, wide = q_ref.shape
+    padded_ref[:OWN, :] = jnp.zeros((OWN, wide), f32)
+    for index, (ref, out_ref) in enumerate(((q_ref, fq_ref), (k_ref, fk_ref), (v_ref, fv_ref))):
+        padded_ref[OWN:, :] = ref[...].astype(f32)
+        for column in range(0, wide, LANES):
+            part = slice(column, column + LANES)
+            total = w_ref[index, 0:1, part] * padded_ref[OWN:, part]
+            for j in range(1, TAPS):
+                total = total + w_ref[index, j : j + 1, part] * padded_ref[OWN - j : OWN - j + rows, part]
+            out_ref[:, part] = total
+
+
+def unpack_kernel(
+    in_ref,
+    fq_ref,
+    fk_ref,
+    fv_ref,
+    c_ref,
+    w_ref,
+    mixed_ref,
+    qg_ref,
+    kg_ref,
+    vg_ref,
+    fg_ref,
+    wg_ref,
+    conv_ref,
+    grad_ref,
+    edge_ref,
+    first_ref,
+    padded_ref,
+):
     wide = in_ref.shape[0] * 2
+    rows = c_ref.shape[0]
 
     def turned(index):
-        rows = in_ref[:, :, index * LANES : (index + 1) * LANES].reshape(wide, LANES)
-        return rows.astype(f32).T
-
-    for index, ref in enumerate((mixed_ref, qg_ref, kg_ref, vg_ref)):
-        ref[...] = turned(index).astype(bf16)
-    taps_grad = turned(4)
+        values = in_ref[:, :, index * LANES : (index + 1) * LANES].reshape(wide, LANES)
+        return values.astype(f32).T
+
+    conv_ref[...] = turned(0)
+    grad_ref[...] = turned(1)
+    taps_grad = turned(2)
     for g in range(GROUPS):
         fg_ref[:, g * wide : (g + 1) * wide] = taps_grad[g * PIECE : (g + 1) * PIECE]
-    sums = turned(5)
-    total = sums[0:24] + sums[32:56]
+    edge_ref[:LANES, :] = turned(3)
+    total = edge_ref[0:24, :] + edge_ref[32:56, :]
     for index in range(3):
         wg_ref[index] = total[TAPS * index : TAPS * (index + 1)]
+
+    last = slice(LANES, LANES + OWN)
+    after = slice(LANES + OWN, LANES + 2 * OWN)
+    edge_ref[after, :] = jnp.zeros((OWN, wide), f32)
+    for index, ref in enumerate((fq_ref, fk_ref, fv_ref)):
+        edge_ref[last, :] = edge_ref[96 + OWN * index : 96 + OWN * (index + 1), :]
+        first = ref[:OWN, :]
+        for j in range(1, TAPS):
+            start = LANES + OWN - j
+            first = first + w_ref[index, j : j + 1, :] * edge_ref[start : start + OWN, :]
+        first_ref[index] = first
+
+    def feat(index, part):
+        ref = (fq_ref, fk_ref, fv_ref)[index]
+        return jnp.concatenate([first_ref[index, :, part], ref[OWN:, part]], axis=0)
+
+    for index, out_ref in enumerate((qg_ref, kg_ref, vg_ref)):
+        padded_ref[rows:, :] = edge_ref[64 + OWN * index : 64 + OWN * (index + 1), :]
+        for column in range(0, wide, LANES):
+            part = slice(column, column + LANES)
+            if index == 0:
+                conv = conv_ref[:, part]
+                mixed_ref[:, part] = (feat(0, part) * conv).astype(bf16)
+                grad = c_ref[:, part].astype(f32) * conv
+            else:
+                grad = grad_ref[:, part] * feat(3 - index, part)
+            padded_ref[:rows, part] = grad
+            total = w_ref[index, 0:1, part] * grad
+            for j in range(1, TAPS):
+                total = total + w_ref[index, j : j + 1, part] * padded_ref[j : j + rows, part]
+            out_ref[:, part] = total.astype(bf16)
 
 
 def owner_kernel(
@@ -252,41 +315,38 @@
 
     @pl.loop(0, steps, unroll=16)
     def _(step):
-        mixed, taps_grad = [], []
+        convs, mix_grads, taps_grad = [], [], []
         for which in range(4):
             s = step * 4 + which
             conv = mix_ref[block_rows(s), :].astype(bf16).astype(f32)
             mix_ref[block_rows(s), :] = conv
-            mixed.append(feat_ref[0, s] * conv)
+            convs.append(conv)
+            mix_grads.append(res_ref[back_block(s), :])
             taps_grad.append(swap_pieces(gate_ref[back_block(s), :]))
-        put(step, 0, mixed)
-        put(step, 4, taps_grad)
+        put(step, 0, convs)
+        put(step, 1, mix_grads)
+        put(step, 2, taps_grad)
+
+    def grad_of(index, s):
+        if index == 0:
+            return raw_ref[3, s] * mix_ref[block_rows(s), :]
+        return res_ref[back_block(s), :] * feat_ref[3 - index, s]
 
     all_sums = []
     for index in range(3):
 
         def backward(count, carry, index=index):
             kept, sums = carry
-            for sub in reversed(range(64 // 4)):
-                step = (blocks // 64 - 1 - count) * (64 // 4) + sub
-                grads = [None] * 4
-                for which in (3, 2, 1, 0):
-                    s = step * 4 + which
-                    if index == 0:
-                        grad = raw_ref[3, s] * mix_ref[block_rows(s), :]
-                    else:
-                        grad = res_ref[back_block(s), :] * feat_ref[3 - index, s]
-                    raw = raw_ref[index, s]
-                    rolled = tuple(pltpu.roll(grad, LANES - j, 1) for j in range(1, TAPS))
-                    terms = [w_ref[index * TAPS] * grad]
-                    new_sums = [sums[0] + raw * grad]
-                    for j in range(1, TAPS):
-                        shifted = jnp.where(lane < LANES - j, rolled[j - 1], kept[j - 1])
-                        terms.append(w_ref[index * TAPS + j] * shifted)
-                        new_sums.append(sums[j] + raw * shifted)
-                    kept, sums = rolled, tuple(new_sums)
-                    grads[which] = summed(terms)
-                put(step, index + 1, grads)
+            for which in reversed(range(64)):
+                s = (blocks // 64 - 1 - count) * 64 + which
+                grad = grad_of(index, s)
+                raw = raw_ref[index, s]
+                rolled = tuple(pltpu.roll(grad, LANES - j, 1) for j in range(1, TAPS))
+                new_sums = [sums[0] + raw * grad]
+                for j in range(1, TAPS):
+                    shifted = jnp.where(lane < LANES - j, rolled[j - 1], kept[j - 1])
+                    new_sums.append(sums[j] + raw * shifted)
+                kept, sums = rolled, tuple(new_sums)
             return kept, sums
 
         _, sums = lax.fori_loop(
@@ -301,10 +361,21 @@
         coarse = total.astype(bf16).astype(f32)
         high = jnp.where(lane == index, coarse, high)
         low = jnp.where(lane == index + 32, total - coarse, low)
-    both = [high + low] * 4
-
+    both = high + low
+    octet = lane // OWN
     for step in range(steps):
-        put(step, 5, both)
+        edges = []
+        for s in range(step * 4, step * 4 + 4):
+            edge = both
+            for index in range(3):
+                if s + 1 < blocks:
+                    head = pltpu.roll(grad_of(index, s + 1), 64 + OWN * index, 1)
+                    edge = jnp.where(octet == 8 + index, head, edge)
+                if s > 0:
+                    tail = pltpu.roll(raw_ref[index, s - 1], 96 + OWN + OWN * index, 1)
+                    edge = jnp.where(octet == 12 + index, tail, edge)
+            edges.append(edge)
+        put(step, 3, edges)
 
 
 def on_device(query_raw, key_raw, value_raw, featurizer, filter_taps, cotangent):
@@ -327,6 +398,16 @@
     )(*sources)
     received = lax.all_to_all(packed, SEQ_CH, split_axis=0, concat_axis=0, tiled=True)
 
+    feat = jax.ShapeDtypeStruct((tok_rows, channels), f32)
+    feats = pl.pallas_call(
+        feat_kernel,
+        out_shape=(feat,) * 3,
+        scratch_shapes=[pltpu.VMEM((tok_rows + OWN, channels), f32)],
+        compiler_params=small,
+        cost_estimate=pl.CostEstimate(flops=3000000, bytes_accessed=1200000, transcendentals=0),
+        name="feat",
+    )(query_raw, key_raw, value_raw, featurizer)
+
     weights = lax.all_gather(featurizer, "ch")
     weights = lax.dynamic_slice(weights, (0, 0, 0, 2 * me), (GROUPS, 3, TAPS, 2))
     weights = weights.transpose(0, 3, 1, 2).reshape(OWN, 3 * TAPS)
@@ -335,7 +416,7 @@
     by_channel = pltpu.VMEM((OWN, blocks, LANES), f32)
     outgoing = pl.pallas_call(
         functools.partial(owner_kernel, blocks=blocks, scale=(blocks * LANES) ** -0.5),
-        out_shape=jax.ShapeDtypeStruct((devices, 2, 6 * LANES), bf16),
+        out_shape=jax.ShapeDtypeStruct((devices, 2, 4 * LANES), bf16),
         scratch_shapes=[
             pltpu.VMEM((3 * TAPS, OWN, LANES), f32),
             pltpu.VMEM((4, blocks, OWN, LANES), f32),
@@ -363,9 +444,16 @@
             jax.ShapeDtypeStruct(filter_taps.shape, f32),
             jax.ShapeDtypeStruct(featurizer.shape, f32),
         ),
+        scratch_shapes=[
+            pltpu.VMEM((tok_rows, channels), f32),
+            pltpu.VMEM((tok_rows, channels), f32),
+            pltpu.VMEM((LANES + 2 * OWN, channels), f32),
+            pltpu.VMEM((3, OWN, channels), f32),
+            pltpu.VMEM((tok_rows + OWN, channels), f32),
+        ],
         compiler_params=small,
         name="unpack",
-    )(returned)
+    )(returned, *feats, cotangent, featurizer)
 
 
 def solution(mesh):

time: 83.8 us -> 81.1 us (0.968)
  blocking collectives: 39.3 us -> 7.92 us
  waiting for transfers between devices: 14.8 us -> 34.8 us
  starting transfers between devices: 15.7 us -> 21.8 us
  Pallas kernels: 12.9 us -> 15.3 us
    all_to_all x1 -> x0, blocking collectives: 31.3 us -> none  [on_device(): lax.all_to_all(outgoing, SEQ_CH, split_axis=0, concat_axis=0, tiled=True)]
    all_to_all x0 -> x1, waiting for transfers between devices: none -> 20 us  [on_device(): lax.all_to_all(outgoing, SEQ_CH, split_axis=0, concat_axis=0, tiled=True)]
    all_to_all x0 -> x1, starting transfers between devices: none -> 6.1 us  [on_device(): lax.all_to_all(outgoing, SEQ_CH, split_axis=0, concat_axis=0, tiled=True)]
    pallas_call x1, Pallas kernels: 1.22 us -> 2.13 us  [on_device(): pl.pallas_call(unpack_kernel, out_shape=(here,) * 4 + (jax.ShapeDtypeStru...]
  transfers between devices with their start and end apart: 1 -> 2, of which waited for: 1 -> 2; matrix products, arithmetic and copies ran while one was open for 0% -> 0% of each run, Pallas kernels for 0% -> 1%
where the time goes in v6:
time: 81.1 us; the launch traced here: 80.9 us
  waiting for transfers between devices  34.8 us (43%)
  starting transfers between devices  21.8 us (27%)
  Pallas kernels  15.3 us (19%)
  blocking collectives  7.92 us (10%)
    all_to_all x1, waiting for transfers between devices, on_device(): lax.all_to_all(outgoing, SEQ_CH, split_axis=0, concat_axis=0, tiled=True)  20 us
    all_to_all x1, starting transfers between devices, on_device(): lax.all_to_all(packed, SEQ_CH, split_axis=0, concat_axis=0, tiled=True)  15.7 us
    all_to_all x1, waiting for transfers between devices, on_device(): lax.all_to_all(packed, SEQ_CH, split_axis=0, concat_axis=0, tiled=True)  14.8 us
    pallas_call x1, Pallas kernels, on_device(): pl.pallas_call(functools.partial(owner_kernel, blocks=blocks, scale=(bloc...  9.91 us
    all_gather x1, blocking collectives, on_device(): weights = lax.all_gather(featurizer, 'ch')  7.92 us
    all_to_all x1, starting transfers between devices, on_device(): lax.all_to_all(outgoing, SEQ_CH, split_axis=0, concat_axis=0, tiled=True)  6.1 us
    pallas_call x1, Pallas kernels, on_device(): pl.pallas_call(pack_kernel, in_specs=[pl.BlockSpec(memory_space=pltpu.Mem...  2.54 us
    pallas_call x1, Pallas kernels, on_device(): pl.pallas_call(unpack_kernel, out_shape=(here,) * 4 + (jax.ShapeDtypeStru...  2.13 us
  transfers between devices with their start and end apart: 2, of which 2 were waited for; matrix products, arithmetic and copies ran while one was open for 0% of the time, Pallas kernels for 1%

profile of v6, /device:TPU:1, one launch (start us, length us, event | category | flops | bytes accessed | tf_op | source)
XLA Modules:
  0.0 80.9 jit_solution(2404630528481134630)
XLA Ops:
  0.6 2.5 %pack.1 = bf16[256,2,640]{2,1,0:T(2,128)(2,1)} custom-call(bf16[128,512]{1,0:T(8,128)(2,1)} %q_ref.1, bf16[128,512]{1,0:T(8,128)(2,1)} %k_ref.1, bf16[128,512]{1,0:T(8,128)(2,1)} %v_ref.1, bf16[128,512]{1,0:T(8,128)(2,1)} %c_ref.1, bf16[32,2048]{1,0:T(8,128)(2,1)} %refs_4_.1), custom_call_target="tpu_custom_call" | custom-call | tf_op jit(solution)/shard_map/pack/pallas_call | solution.py:390
  3.2 0.0 copy-start.4
  3.2 15.7 %all-to-all-start = ((bf16[256,2,640]{2,1,0:T(2,128)(2,1)}), bf16[256,2,640]{2,1,0:T(2,128)(2,1)S(1)}, u32[]{:S(2)}, u32[]{:S(2)}) async-start(bf16[256,2,640]{2,1,0:T(2,128)(2,1)} %pack.1), calls=%async_computation | async-start | bytes 1310720 | tf_op jit(solution)/shard_map/all_to_all | solution.py:399
  18.9 0.0 copy-done.4
  18.9 7.9 %all-gather = f32[12,7,512]{2,1,0:T(8,128)S(1)} all-gather(f32[3,7,512]{2,1,0:T(8,128)S(1)} %copy-done.4), channel_id=2, replica_groups=mesh['seq_0'=2,'seq_1'=8,'seq_2'=4,'ch'=4] {'ch'}, dimensions={0}, use_global_device_ids=true | all-gather | bytes 215040 | tf_op jit(solution)/shard_map/all_gather | solution.py:411
  26.8 0.1 constant_dynamic-slice_fusion
  26.9 0.2 copy.15
  27.1 0.1 reshape.15.own_ref
  27.1 14.8 %all-to-all-done.in_ref = bf16[256,2,640]{2,1,0:T(2,128)(2,1)S(1)} async-done(((bf16[256,2,640]{2,1,0:T(2,128)(2,1)}), bf16[256,2,640]{2,1,0:T(2,128)(2,1)S(1)}, u32[]{:S(2)}, u32[]{:S(2)}) %all-to-all-start) | async-done | bytes 655392 | tf_op jit(solution)/shard_map/all_to_all | solution.py:399
  41.9 9.9 %owner.1 = bf16[256,2,512]{2,1,0:T(2,128)(2,1)} custom-call(bf16[256,2,640]{2,1,0:T(2,128)(2,1)S(1)} %all-to-all-done.in_ref, f32[8,21]{1,0:T(8,128)S(1)} %reshape.15.own_ref), custom_call_target="tpu_custom_call" | custom-call | tf_op jit(solution)/shard_map/owner/pallas_call | solution.py:417
  51.9 0.0 copy-start
  51.9 0.0 copy-start.1
  51.9 0.0 copy-start.2
  51.9 6.1 %all-to-all-start.1 = ((bf16[256,2,512]{2,1,0:T(2,128)(2,1)}), bf16[256,2,512]{2,1,0:T(2,128)(2,1)S(1)}, u32[]{:S(2)}, u32[]{:S(2)}) async-start(bf16[256,2,512]{2,1,0:T(2,128)(2,1)} %owner.1), calls=%async_computation.1 | async-start | bytes 1048576 | tf_op jit(solution)/shard_map/all_to_all | solution.py:437
  58.0 0.0 copy-done
  58.0 0.0 copy-done.1
  58.0 0.0 copy-done.2
  58.0 0.0 copy-start.3
  58.0 0.7 feat.1
  58.7 20.0 %all-to-all-done.1.in_ref = bf16[256,2,512]{2,1,0:T(2,128)(2,1)S(1)} async-done(((bf16[256,2,512]{2,1,0:T(2,128)(2,1)}), bf16[256,2,512]{2,1,0:T(2,128)(2,1)S(1)}, u32[]{:S(2)}, u32[]{:S(2)}) %all-to-all-start.1) | async-done | bytes 524320 | tf_op jit(solution)/shard_map/all_to_all | solution.py:437
  78.7 0.0 copy-done.3
  78.8 2.1 %unpack.1 = (bf16[128,512]{1,0:T(8,128)(2,1)}, bf16[128,512]{1,0:T(8,128)(2,1)}, bf16[128,512]{1,0:T(8,128)(2,1)}, bf16[128,512]{1,0:T(8,128)(2,1)}, f32[32,2048]{1,0:T(8,128)}, /*index=5*/f32[3,7,512]{2,1,0:T(8,128)}) custom-call(bf16[256,2,512]{2,1,0:T(2,128)(2,1)S(1)} %all-to-all-done.1.in_ref, f32[128,512]{1,0:T(8,128)S(1)} %get-tuple-element.9.fq_ref, ...), custom_call_target="tpu_custom_call" | custom-call | tf_op jit(solution)/shard_map/unpack/pallas_call | solution.py:440
Async XLA Ops:
  3.2 15.7 %copy-start.4 = (f32[3,7,512]{2,1,0:T(8,128)S(1)}, f32[3,7,512]{2,1,0:T(8,128)}, u32[]{:S(2)}) copy-start(f32[3,7,512]{2,1,0:T(8,128)} %w_ref.3) | copy-start | bytes 129028
  3.2 38.8 %all-to-all-start = ((bf16[256,2,640]{2,1,0:T(2,128)(2,1)}), bf16[256,2,640]{2,1,0:T(2,128)(2,1)S(1)}, u32[]{:S(2)}, u32[]{:S(2)}) async-start(bf16[256,2,640]{2,1,0:T(2,128)(2,1)} %pack.1), calls=%async_computation | async-start | bytes 1310720 | tf_op jit(solution)/shard_map/all_to_all | solution.py:399
  51.9 6.1 %copy-start = (bf16[128,512]{1,0:T(8,128)(2,1)S(1)}, bf16[128,512]{1,0:T(8,128)(2,1)}, u32[]{:S(2)}) copy-start(bf16[128,512]{1,0:T(8,128)(2,1)} %q_ref.1) | copy-start | bytes 393220
  51.9 6.1 %copy-start.1 = (bf16[128,512]{1,0:T(8,128)(2,1)S(1)}, bf16[128,512]{1,0:T(8,128)(2,1)}, u32[]{:S(2)}) copy-start(bf16[128,512]{1,0:T(8,128)(2,1)} %k_ref.1) | copy-start | bytes 393220
  51.9 6.1 %copy-start.2 = (bf16[128,512]{1,0:T(8,128)(2,1)S(1)}, bf16[128,512]{1,0:T(8,128)(2,1)}, u32[]{:S(2)}) copy-start(bf16[128,512]{1,0:T(8,128)(2,1)} %v_ref.1) | copy-start | bytes 393220
  51.9 26.9 %all-to-all-start.1 = ((bf16[256,2,512]{2,1,0:T(2,128)(2,1)}), bf16[256,2,512]{2,1,0:T(2,128)(2,1)S(1)}, u32[]{:S(2)}, u32[]{:S(2)}) async-start(bf16[256,2,512]{2,1,0:T(2,128)(2,1)} %owner.1), calls=%async_computation.1 | async-start | bytes 1048576 | tf_op jit(solution)/shard_map/all_to_all | solution.py:437
  58.0 20.8 %copy-start.3 = (bf16[128,512]{1,0:T(8,128)(2,1)S(1)}, bf16[128,512]{1,0:T(8,128)(2,1)}, u32[]{:S(2)}) copy-start(bf16[128,512]{1,0:T(8,128)(2,1)} %c_ref.1) | copy-start | bytes 393220

commit v7 on v6

--- a/solution.py
+++ b/solution.py
@@ -64,20 +64,19 @@
     fv_ref,
     c_ref,
     w_ref,
-    mixed_ref,
-    qg_ref,
-    kg_ref,
-    vg_ref,
-    fg_ref,
-    wg_ref,
-    conv_ref,
-    grad_ref,
-    edge_ref,
-    first_ref,
-    padded_ref,
+    *refs,
 ):
+    results, ready = refs[:6], refs[6:12]
+    mixed_ref, qg_ref, kg_ref, vg_ref, fg_ref, wg_ref = ready
+    conv_ref, grad_ref, edge_ref, first_ref, padded_ref, sems = refs[12:]
     wide = in_ref.shape[0] * 2
     rows = c_ref.shape[0]
+
+    sends = []
+
+    def send(index):
+        sends.append(pltpu.make_async_copy(ready[index], results[index], sems.at[index]))
+        sends[-1].start()
 
     def turned(index):
         values = in_ref[:, :, index * LANES : (index + 1) * LANES].reshape(wide, LANES)
@@ -88,16 +87,18 @@
     taps_grad = turned(2)
     for g in range(GROUPS):
         fg_ref[:, g * wide : (g + 1) * wide] = taps_grad[g * PIECE : (g + 1) * PIECE]
+    send(4)
     edge_ref[:LANES, :] = turned(3)
     total = edge_ref[0:24, :] + edge_ref[32:56, :]
     for index in range(3):
         wg_ref[index] = total[TAPS * index : TAPS * (index + 1)]
+    send(5)
 
     last = slice(LANES, LANES + OWN)
     after = slice(LANES + OWN, LANES + 2 * OWN)
     edge_ref[after, :] = jnp.zeros((OWN, wide), f32)
     for index, ref in enumerate((fq_ref, fk_ref, fv_ref)):
-        edge_ref[last, :] = edge_ref[96 + OWN * index : 96 + OWN * (index + 1), :]
+        edge_ref[last, :] = edge_ref[56 + 2 * OWN * index : 64 + 2 * OWN * index, :]
         first = ref[:OWN, :]
         for j in range(1, TAPS):
             start = LANES + OWN - j
@@ -109,7 +110,7 @@
         return jnp.concatenate([first_ref[index, :, part], ref[OWN:, part]], axis=0)
 
     for index, out_ref in enumerate((qg_ref, kg_ref, vg_ref)):
-        padded_ref[rows:, :] = edge_ref[64 + OWN * index : 64 + OWN * (index + 1), :]
+        padded_ref[rows:, :] = edge_ref[64 + 2 * OWN * index : 72 + 2 * OWN * index, :]
         for column in range(0, wide, LANES):
             part = slice(column, column + LANES)
             if index == 0:
@@ -123,6 +124,11 @@
             for j in range(1, TAPS):
                 total = total + w_ref[index, j : j + 1, part] * padded_ref[j : j + rows, part]
             out_ref[:, part] = total.astype(bf16)
+        if index == 0:
+            send(0)
+        send(index + 1)
+    for one in sends:
+        one.wait()
 
 
 def owner_kernel(
@@ -362,18 +368,16 @@
         high = jnp.where(lane == index, coarse, high)
         low = jnp.where(lane == index + 32, total - coarse, low)
     both = high + low
-    octet = lane // OWN
+    last_octet = lane >= LANES - OWN
     for step in range(steps):
         edges = []
         for s in range(step * 4, step * 4 + 4):
             edge = both
             for index in range(3):
-                if s + 1 < blocks:
-                    head = pltpu.roll(grad_of(index, s + 1), 64 + OWN * index, 1)
-                    edge = jnp.where(octet == 8 + index, head, edge)
-                if s > 0:
-                    tail = pltpu.roll(raw_ref[index, s - 1], 96 + OWN + OWN * index, 1)
-                    edge = jnp.where(octet == 12 + index, tail, edge)
+                head = grad_of(index, s + 1) if s + 1 < blocks else zero
+                tail = raw_ref[index, s - 1] if s > 0 else zero
+                ends = pltpu.roll(jnp.where(last_octet, tail, head), 64 + 2 * OWN * index, 1)
+                edge = jnp.where((lane + OWN) // (2 * OWN) == 4 + index, ends, edge)
             edges.append(edge)
         put(step, 3, edges)
 
@@ -437,19 +441,22 @@
     returned = lax.all_to_all(outgoing, SEQ_CH, split_axis=0, concat_axis=0, tiled=True)
 
     here = jax.ShapeDtypeStruct((tok_rows, channels), bf16)
+    results = (here,) * 4 + (
+        jax.ShapeDtypeStruct(filter_taps.shape, f32),
+        jax.ShapeDtypeStruct(featurizer.shape, f32),
+    )
     return pl.pallas_call(
         unpack_kernel,
-        out_shape=(here,) * 4
-        + (
-            jax.ShapeDtypeStruct(filter_taps.shape, f32),
-            jax.ShapeDtypeStruct(featurizer.shape, f32),
-        ),
-        scratch_shapes=[
+        out_specs=[pl.BlockSpec(memory_space=pltpu.MemorySpace.HBM)] * len(results),
+        out_shape=results,
+        scratch_shapes=[pltpu.VMEM(result.shape, result.dtype) for result in results]
+        + [
             pltpu.VMEM((tok_rows, channels), f32),
             pltpu.VMEM((tok_rows, channels), f32),
             pltpu.VMEM((LANES + 2 * OWN, channels), f32),
             pltpu.VMEM((3, OWN, channels), f32),
             pltpu.VMEM((tok_rows + OWN, channels), f32),
+            pltpu.SemaphoreType.DMA((len(results),)),
         ],
         compiler_params=small,
         name="unpack",

time: 81.1 us -> 81 us (level)
  no operation moved by 1% of the time
where the time goes in v7:
time: 81 us; the launch traced here: 80.8 us
  waiting for transfers between devices  34.8 us (43%)
  starting transfers between devices  21.8 us (27%)
  Pallas kernels  15.2 us (19%)
  blocking collectives  7.92 us (10%)
    all_to_all x1, waiting for transfers between devices, on_device(): lax.all_to_all(outgoing, SEQ_CH, split_axis=0, concat_axis=0, tiled=True)  20 us
    all_to_all x1, starting transfers between devices, on_device(): lax.all_to_all(packed, SEQ_CH, split_axis=0, concat_axis=0, tiled=True)  15.7 us
    all_to_all x1, waiting for transfers between devices, on_device(): lax.all_to_all(packed, SEQ_CH, split_axis=0, concat_axis=0, tiled=True)  14.8 us
    pallas_call x1, Pallas kernels, on_device(): pl.pallas_call(functools.partial(owner_kernel, blocks=blocks, scale=(bloc...  9.83 us
    all_gather x1, blocking collectives, on_device(): weights = lax.all_gather(featurizer, 'ch')  7.92 us
    all_to_all x1, starting transfers between devices, on_device(): lax.all_to_all(outgoing, SEQ_CH, split_axis=0, concat_axis=0, tiled=True)  6.1 us
    pallas_call x1, Pallas kernels, on_device(): pl.pallas_call(pack_kernel, in_specs=[pl.BlockSpec(memory_space=pltpu.Mem...  2.54 us
    pallas_call x1, Pallas kernels, on_device(): pl.pallas_call(unpack_kernel, out_specs=[pl.BlockSpec(memory_space=pltpu....  2.09 us
  transfers between devices with their start and end apart: 2, of which 2 were waited for; matrix products, arithmetic and copies ran while one was open for 0% of the time, Pallas kernels for 1%

profile of v7, /device:TPU:1, one launch (start us, length us, event | category | flops | bytes accessed | tf_op | source)
XLA Modules:
  0.0 80.8 jit_solution(5069272407018993287)
XLA Ops:
  0.6 2.5 %pack.1 = bf16[256,2,640]{2,1,0:T(2,128)(2,1)} custom-call(bf16[128,512]{1,0:T(8,128)(2,1)} %q_ref.1, bf16[128,512]{1,0:T(8,128)(2,1)} %k_ref.1, bf16[128,512]{1,0:T(8,128)(2,1)} %v_ref.1, bf16[128,512]{1,0:T(8,128)(2,1)} %c_ref.1, bf16[32,2048]{1,0:T(8,128)(2,1)} %refs_4_.1), custom_call_target="tpu_custom_call" | custom-call | tf_op jit(solution)/shard_map/pack/pallas_call | solution.py:394
  3.2 0.0 copy-start.4
  3.2 15.7 %all-to-all-start = ((bf16[256,2,640]{2,1,0:T(2,128)(2,1)}), bf16[256,2,640]{2,1,0:T(2,128)(2,1)S(1)}, u32[]{:S(2)}, u32[]{:S(2)}) async-start(bf16[256,2,640]{2,1,0:T(2,128)(2,1)} %pack.1), calls=%async_computation | async-start | bytes 1310720 | tf_op jit(solution)/shard_map/all_to_all | solution.py:403
  18.9 0.0 copy-done.4
  18.9 7.9 %all-gather = f32[12,7,512]{2,1,0:T(8,128)S(1)} all-gather(f32[3,7,512]{2,1,0:T(8,128)S(1)} %copy-done.4), channel_id=2, replica_groups=mesh['seq_0'=2,'seq_1'=8,'seq_2'=4,'ch'=4] {'ch'}, dimensions={0}, use_global_device_ids=true | all-gather | bytes 215040 | tf_op jit(solution)/shard_map/all_gather | solution.py:415
  26.8 0.1 constant_dynamic-slice_fusion
  26.9 0.2 copy.15
  27.1 0.1 reshape.15.own_ref
  27.1 14.8 %all-to-all-done.in_ref = bf16[256,2,640]{2,1,0:T(2,128)(2,1)S(1)} async-done(((bf16[256,2,640]{2,1,0:T(2,128)(2,1)}), bf16[256,2,640]{2,1,0:T(2,128)(2,1)S(1)}, u32[]{:S(2)}, u32[]{:S(2)}) %all-to-all-start) | async-done | bytes 655392 | tf_op jit(solution)/shard_map/all_to_all | solution.py:403
  41.9 9.8 %owner.1 = bf16[256,2,512]{2,1,0:T(2,128)(2,1)} custom-call(bf16[256,2,640]{2,1,0:T(2,128)(2,1)S(1)} %all-to-all-done.in_ref, f32[8,21]{1,0:T(8,128)S(1)} %reshape.15.own_ref), custom_call_target="tpu_custom_call" | custom-call | tf_op jit(solution)/shard_map/owner/pallas_call | solution.py:421
  51.8 0.0 copy-start
  51.8 0.0 copy-start.1
  51.8 0.0 copy-start.2
  51.8 6.1 %all-to-all-start.1 = ((bf16[256,2,512]{2,1,0:T(2,128)(2,1)}), bf16[256,2,512]{2,1,0:T(2,128)(2,1)S(1)}, u32[]{:S(2)}, u32[]{:S(2)}) async-start(bf16[256,2,512]{2,1,0:T(2,128)(2,1)} %owner.1), calls=%async_computation.1 | async-start | bytes 1048576 | tf_op jit(solution)/shard_map/all_to_all | solution.py:441
  57.9 0.0 copy-done
  57.9 0.0 copy-done.1
  57.9 0.0 copy-done.2
  57.9 0.0 copy-start.3
  57.9 0.7 feat.1
  58.7 20.0 %all-to-all-done.1.in_ref = bf16[256,2,512]{2,1,0:T(2,128)(2,1)S(1)} async-done(((bf16[256,2,512]{2,1,0:T(2,128)(2,1)}), bf16[256,2,512]{2,1,0:T(2,128)(2,1)S(1)}, u32[]{:S(2)}, u32[]{:S(2)}) %all-to-all-start.1) | async-done | bytes 524320 | tf_op jit(solution)/shard_map/all_to_all | solution.py:441
  78.7 0.0 copy-done.3
  78.7 2.1 %unpack.1 = (bf16[128,512]{1,0:T(8,128)(2,1)}, bf16[128,512]{1,0:T(8,128)(2,1)}, bf16[128,512]{1,0:T(8,128)(2,1)}, bf16[128,512]{1,0:T(8,128)(2,1)}, f32[32,2048]{1,0:T(8,128)}, /*index=5*/f32[3,7,512]{2,1,0:T(8,128)}) custom-call(bf16[256,2,512]{2,1,0:T(2,128)(2,1)S(1)} %all-to-all-done.1.in_ref, f32[128,512]{1,0:T(8,128)S(1)} %get-tuple-element.9.fq_ref, ...), custom_call_target="tpu_custom_call" | custom-call | tf_op jit(solution)/shard_map/unpack/pallas_call | solution.py:448
Async XLA Ops:
  3.2 15.7 %copy-start.4 = (f32[3,7,512]{2,1,0:T(8,128)S(1)}, f32[3,7,512]{2,1,0:T(8,128)}, u32[]{:S(2)}) copy-start(f32[3,7,512]{2,1,0:T(8,128)} %w_ref.3) | copy-start | bytes 129028
  3.2 38.8 %all-to-all-start = ((bf16[256,2,640]{2,1,0:T(2,128)(2,1)}), bf16[256,2,640]{2,1,0:T(2,128)(2,1)S(1)}, u32[]{:S(2)}, u32[]{:S(2)}) async-start(bf16[256,2,640]{2,1,0:T(2,128)(2,1)} %pack.1), calls=%async_computation | async-start | bytes 1310720 | tf_op jit(solution)/shard_map/all_to_all | solution.py:403
  51.8 6.1 %copy-start = (bf16[128,512]{1,0:T(8,128)(2,1)S(1)}, bf16[128,512]{1,0:T(8,128)(2,1)}, u32[]{:S(2)}) copy-start(bf16[128,512]{1,0:T(8,128)(2,1)} %q_ref.1) | copy-start | bytes 393220
  51.8 6.1 %copy-start.1 = (bf16[128,512]{1,0:T(8,128)(2,1)S(1)}, bf16[128,512]{1,0:T(8,128)(2,1)}, u32[]{:S(2)}) copy-start(bf16[128,512]{1,0:T(8,128)(2,1)} %k_ref.1) | copy-start | bytes 393220
  51.8 6.1 %copy-start.2 = (bf16[128,512]{1,0:T(8,128)(2,1)S(1)}, bf16[128,512]{1,0:T(8,128)(2,1)}, u32[]{:S(2)}) copy-start(bf16[128,512]{1,0:T(8,128)(2,1)} %v_ref.1) | copy-start | bytes 393220
  51.8 26.9 %all-to-all-start.1 = ((bf16[256,2,512]{2,1,0:T(2,128)(2,1)}), bf16[256,2,512]{2,1,0:T(2,128)(2,1)S(1)}, u32[]{:S(2)}, u32[]{:S(2)}) async-start(bf16[256,2,512]{2,1,0:T(2,128)(2,1)} %owner.1), calls=%async_computation.1 | async-start | bytes 1048576 | tf_op jit(solution)/shard_map/all_to_all | solution.py:441
  57.9 20.8 %copy-start.3 = (bf16[128,512]{1,0:T(8,128)(2,1)S(1)}, bf16[128,512]{1,0:T(8,128)(2,1)}, u32[]{:S(2)}) copy-start(bf16[128,512]{1,0:T(8,128)(2,1)} %c_ref.1) | copy-start | bytes 393220

commit v8 on v7

--- a/solution.py
+++ b/solution.py
@@ -24,6 +24,7 @@
 
 def pack_kernel(*refs):
     sources, out_ref, copies, sems = refs[:5], refs[5], refs[6:11], refs[11]
+    ready_ref, sent_sems = refs[12:]
     moves = [
         pltpu.make_async_copy(source, copy, sems.at[index])
         for index, (source, copy) in enumerate(zip(sources, copies))
@@ -33,8 +34,13 @@
     pairs = (out_ref.shape[0], 2, LANES)
     wide = out_ref.shape[0] * 2
 
+    sends = []
+
     def put(index, rows):
-        out_ref[:, :, index * LANES : (index + 1) * LANES] = rows.T.astype(bf16).reshape(pairs)
+        ready_ref[index] = rows.T.astype(bf16).reshape(pairs)
+        place = out_ref.at[:, :, index * LANES : (index + 1) * LANES]
+        sends.append(pltpu.make_async_copy(ready_ref.at[index], place, sent_sems.at[index]))
+        sends[index].start()
 
     for index in range(4):
         moves[index].wait()
@@ -42,6 +48,8 @@
     moves[4].wait()
     taps = copies[4][...].astype(f32)
     put(4, jnp.concatenate([taps[:, g * wide : (g + 1) * wide] for g in range(GROUPS)], axis=0))
+    for send in sends:
+        send.wait()
 
 
 def feat_kernel(q_ref, k_ref, v_ref, w_ref, fq_ref, fk_ref, fv_ref, padded_ref):
@@ -394,9 +402,14 @@
     packed = pl.pallas_call(
         pack_kernel,
         in_specs=[pl.BlockSpec(memory_space=pltpu.MemorySpace.HBM)] * len(sources),
+        out_specs=pl.BlockSpec(memory_space=pltpu.MemorySpace.HBM),
         out_shape=jax.ShapeDtypeStruct((devices, 2, 5 * LANES), bf16),
         scratch_shapes=[pltpu.VMEM(source.shape, source.dtype) for source in sources]
-        + [pltpu.SemaphoreType.DMA((len(sources),))],
+        + [
+            pltpu.SemaphoreType.DMA((len(sources),)),
+            pltpu.VMEM((len(sources), devices, 2, LANES), bf16),
+            pltpu.SemaphoreType.DMA((len(sources),)),
+        ],
         compiler_params=pltpu.CompilerParams(vmem_limit_bytes=60 * MIB),
         name="pack",
     )(*sources)

time: 81 us -> 80.9 us (level)
  no operation moved by 1% of the time
where the time goes in v8:
time: 80.9 us; the launch traced here: 80.7 us
  waiting for transfers between devices  34.8 us (43%)
  starting transfers between devices  21.8 us (27%)
  Pallas kernels  15.1 us (19%)
  blocking collectives  7.92 us (10%)
    all_to_all x1, waiting for transfers between devices, on_device(): lax.all_to_all(outgoing, SEQ_CH, split_axis=0, concat_axis=0, tiled=True)  20 us
    all_to_all x1, starting transfers between devices, on_device(): lax.all_to_all(packed, SEQ_CH, split_axis=0, concat_axis=0, tiled=True)  15.7 us
    all_to_all x1, waiting for transfers between devices, on_device(): lax.all_to_all(packed, SEQ_CH, split_axis=0, concat_axis=0, tiled=True)  14.8 us
    pallas_call x1, Pallas kernels, on_device(): pl.pallas_call(functools.partial(owner_kernel, blocks=blocks, scale=(bloc...  9.83 us
    all_gather x1, blocking collectives, on_device(): weights = lax.all_gather(featurizer, 'ch')  7.92 us
    all_to_all x1, starting transfers between devices, on_device(): lax.all_to_all(outgoing, SEQ_CH, split_axis=0, concat_axis=0, tiled=True)  6.09 us
    pallas_call x1, Pallas kernels, on_device(): pl.pallas_call(pack_kernel, in_specs=[pl.BlockSpec(memory_space=pltpu.Mem...  2.43 us
    pallas_call x1, Pallas kernels, on_device(): pl.pallas_call(unpack_kernel, out_specs=[pl.BlockSpec(memory_space=pltpu....  2.09 us
  transfers between devices with their start and end apart: 2, of which 2 were waited for; matrix products, arithmetic and copies ran while one was open for 0% of the time, Pallas kernels for 1%

profile of v8, /device:TPU:1, one launch (start us, length us, event | category | flops | bytes accessed | tf_op | source)
XLA Modules:
  0.0 80.7 jit_solution(4084416953769270903)
XLA Ops:
  0.6 2.4 %pack.1 = bf16[256,2,640]{2,1,0:T(2,128)(2,1)} custom-call(bf16[128,512]{1,0:T(8,128)(2,1)} %q_ref.1, bf16[128,512]{1,0:T(8,128)(2,1)} %k_ref.1, bf16[128,512]{1,0:T(8,128)(2,1)} %v_ref.1, bf16[128,512]{1,0:T(8,128)(2,1)} %c_ref.1, bf16[32,2048]{1,0:T(8,128)(2,1)} %refs_4_.1), custom_call_target="tpu_custom_call" | custom-call | tf_op jit(solution)/shard_map/pack/pallas_call | solution.py:402
  3.1 0.0 copy-start.4
  3.1 15.7 %all-to-all-start = ((bf16[256,2,640]{2,1,0:T(2,128)(2,1)}), bf16[256,2,640]{2,1,0:T(2,128)(2,1)S(1)}, u32[]{:S(2)}, u32[]{:S(2)}) async-start(bf16[256,2,640]{2,1,0:T(2,128)(2,1)} %pack.1), calls=%async_computation | async-start | bytes 1310720 | tf_op jit(solution)/shard_map/all_to_all | solution.py:416
  18.8 0.0 copy-done.4
  18.8 7.9 %all-gather = f32[12,7,512]{2,1,0:T(8,128)S(1)} all-gather(f32[3,7,512]{2,1,0:T(8,128)S(1)} %copy-done.4), channel_id=2, replica_groups=mesh['seq_0'=2,'seq_1'=8,'seq_2'=4,'ch'=4] {'ch'}, dimensions={0}, use_global_device_ids=true | all-gather | bytes 215040 | tf_op jit(solution)/shard_map/all_gather | solution.py:428
  26.7 0.1 constant_dynamic-slice_fusion
  26.8 0.2 copy.15
  27.0 0.1 reshape.15.own_ref
  27.0 14.8 %all-to-all-done.in_ref = bf16[256,2,640]{2,1,0:T(2,128)(2,1)S(1)} async-done(((bf16[256,2,640]{2,1,0:T(2,128)(2,1)}), bf16[256,2,640]{2,1,0:T(2,128)(2,1)S(1)}, u32[]{:S(2)}, u32[]{:S(2)}) %all-to-all-start) | async-done | bytes 655392 | tf_op jit(solution)/shard_map/all_to_all | solution.py:416
  41.8 9.8 %owner.1 = bf16[256,2,512]{2,1,0:T(2,128)(2,1)} custom-call(bf16[256,2,640]{2,1,0:T(2,128)(2,1)S(1)} %all-to-all-done.in_ref, f32[8,21]{1,0:T(8,128)S(1)} %reshape.15.own_ref), custom_call_target="tpu_custom_call" | custom-call | tf_op jit(solution)/shard_map/owner/pallas_call | solution.py:434
  51.7 0.0 copy-start
  51.7 0.0 copy-start.1
  51.7 0.0 copy-start.2
  51.7 6.1 %all-to-all-start.1 = ((bf16[256,2,512]{2,1,0:T(2,128)(2,1)}), bf16[256,2,512]{2,1,0:T(2,128)(2,1)S(1)}, u32[]{:S(2)}, u32[]{:S(2)}) async-start(bf16[256,2,512]{2,1,0:T(2,128)(2,1)} %owner.1), calls=%async_computation.1 | async-start | bytes 1048576 | tf_op jit(solution)/shard_map/all_to_all | solution.py:454
  57.8 0.0 copy-done
  57.8 0.0 copy-done.1
  57.8 0.0 copy-done.2
  57.8 0.0 copy-start.3
  57.8 0.7 feat.1
  58.6 20.0 %all-to-all-done.1.in_ref = bf16[256,2,512]{2,1,0:T(2,128)(2,1)S(1)} async-done(((bf16[256,2,512]{2,1,0:T(2,128)(2,1)}), bf16[256,2,512]{2,1,0:T(2,128)(2,1)S(1)}, u32[]{:S(2)}, u32[]{:S(2)}) %all-to-all-start.1) | async-done | bytes 524320 | tf_op jit(solution)/shard_map/all_to_all | solution.py:454
  78.6 0.0 copy-done.3
  78.6 2.1 %unpack.1 = (bf16[128,512]{1,0:T(8,128)(2,1)}, bf16[128,512]{1,0:T(8,128)(2,1)}, bf16[128,512]{1,0:T(8,128)(2,1)}, bf16[128,512]{1,0:T(8,128)(2,1)}, f32[32,2048]{1,0:T(8,128)}, /*index=5*/f32[3,7,512]{2,1,0:T(8,128)}) custom-call(bf16[256,2,512]{2,1,0:T(2,128)(2,1)S(1)} %all-to-all-done.1.in_ref, f32[128,512]{1,0:T(8,128)S(1)} %get-tuple-element.9.fq_ref, ...), custom_call_target="tpu_custom_call" | custom-call | tf_op jit(solution)/shard_map/unpack/pallas_call | solution.py:461
Async XLA Ops:
  3.1 15.7 %copy-start.4 = (f32[3,7,512]{2,1,0:T(8,128)S(1)}, f32[3,7,512]{2,1,0:T(8,128)}, u32[]{:S(2)}) copy-start(f32[3,7,512]{2,1,0:T(8,128)} %w_ref.3) | copy-start | bytes 129028
  3.1 38.8 %all-to-all-start = ((bf16[256,2,640]{2,1,0:T(2,128)(2,1)}), bf16[256,2,640]{2,1,0:T(2,128)(2,1)S(1)}, u32[]{:S(2)}, u32[]{:S(2)}) async-start(bf16[256,2,640]{2,1,0:T(2,128)(2,1)} %pack.1), calls=%async_computation | async-start | bytes 1310720 | tf_op jit(solution)/shard_map/all_to_all | solution.py:416
  51.7 6.1 %copy-start = (bf16[128,512]{1,0:T(8,128)(2,1)S(1)}, bf16[128,512]{1,0:T(8,128)(2,1)}, u32[]{:S(2)}) copy-start(bf16[128,512]{1,0:T(8,128)(2,1)} %q_ref.1) | copy-start | bytes 393220
  51.7 6.1 %copy-start.1 = (bf16[128,512]{1,0:T(8,128)(2,1)S(1)}, bf16[128,512]{1,0:T(8,128)(2,1)}, u32[]{:S(2)}) copy-start(bf16[128,512]{1,0:T(8,128)(2,1)} %k_ref.1) | copy-start | bytes 393220
  51.7 6.1 %copy-start.2 = (bf16[128,512]{1,0:T(8,128)(2,1)S(1)}, bf16[128,512]{1,0:T(8,128)(2,1)}, u32[]{:S(2)}) copy-start(bf16[128,512]{1,0:T(8,128)(2,1)} %v_ref.1) | copy-start | bytes 393220
  51.7 26.9 %all-to-all-start.1 = ((bf16[256,2,512]{2,1,0:T(2,128)(2,1)}), bf16[256,2,512]{2,1,0:T(2,128)(2,1)S(1)}, u32[]{:S(2)}, u32[]{:S(2)}) async-start(bf16[256,2,512]{2,1,0:T(2,128)(2,1)} %owner.1), calls=%async_computation.1 | async-start | bytes 1048576 | tf_op jit(solution)/shard_map/all_to_all | solution.py:454
  57.8 20.8 %copy-start.3 = (bf16[128,512]{1,0:T(8,128)(2,1)S(1)}, bf16[128,512]{1,0:T(8,128)(2,1)}, u32[]{:S(2)}) copy-start(bf16[128,512]{1,0:T(8,128)(2,1)} %c_ref.1) | copy-start | bytes 393220
